TPU v7x, 32 devices: a whole 2x2x4 slice. The times are simulated.
32 devices in a mesh: px: 8 (over z, x), py: 4 (over y, core).
Axes of the slice: x: 2, y: 2, z: 4, core: 2. Of those that a mesh axis runs over, the one named last changes fastest.
Arguments:
- conserved: float32 [2, 2, 2, 2, 32, 32, 128], P(None, None, None, None, 'px', 'py'), may hold values from 0.075 to 36
- velocity: float32 [3, 3, 3, 3, 32, 32, 128], P(None, None, None, None, 'px', 'py'), may hold values from -6 to 6
- targets: float32 [2], replicated, may hold values from 0.5 to 2
- handoff_blocks: int32 [8, 32], P('px', 'py'), may hold values from 0 to 31, as said below
- handoff_owner: int32 [8, 32, 1], P('px', 'py'), may hold values from 0 to 3; in each aligned block of 8 rows (0 to 7, 8 to 15, ..., all dimensions but the last counted through in order) at most 4 rows name the same one
Outputs:
- fixed_state: float32 [2, 2, 2, 2, 32, 32, 128], P(None, None, None, None, 'px', 'py')
- handed: float32 [8, 64, 16, 128], P('px', 'py')
Inputs may be any that keep to these rules, and one draw needn't show every extreme that they name: `handoff_blocks`: within one device's 8 entries the column numbers are distinct; column b is the local zone column (b // 8, b % 8). `handoff_owner`: owners are indices along py within the same px group; at most 4 of one device's entries name the same owner, and in some device one owner is named exactly 4 times.
All inputs are finite; a program needn't handle non-finite values.
Results may differ from a plain program's by a relative error of at most 0.00035.
Values sent between devices are 32-bit elements; how exact they have to be, the bound alone decides.
No kernel may reach another device: no remote copies, remote signals or barrier semaphores. Data moves between devices by JAX's collectives and lax.ppermute only.
A program may use at most 64 MiB of HBM per device.

v0:
```python
import math

import jax
import jax.numpy as jnp
import numpy as np
from jax import lax
from jax.sharding import PartitionSpec as P

gamma_less = 0.4
force_step = 0.02
advect_step = 0.5
highest = lax.Precision.HIGHEST


def passed_along(x, axis, by):
    size = lax.axis_size(axis)
    pairs = [(i, i + by) for i in range(size) if 0 <= i + by < size]
    return lax.ppermute(x, axis, pairs)


def triple(factor_one, factor_two, factor_three):
    return np.kron(np.kron(factor_one, factor_two), factor_three)


def build_tables():
    offset = 0.5 / math.sqrt(3.0)
    gauss_nodes = np.array([0.5 - offset, 0.5 + offset])
    linear = np.stack([1.0 - gauss_nodes, gauss_nodes], 1)
    quadratic = np.stack(
        [
            2.0 * (gauss_nodes - 0.5) * (gauss_nodes - 1.0),
            -4.0 * gauss_nodes * (gauss_nodes - 1.0),
            2.0 * gauss_nodes * (gauss_nodes - 0.5),
        ],
        1,
    )
    slopes = np.stack(
        [4.0 * gauss_nodes - 3.0, 4.0 - 8.0 * gauss_nodes, 4.0 * gauss_nodes - 1.0], 1
    )
    line_mass = np.array([[1.0 / 3.0, 1.0 / 6.0], [1.0 / 6.0, 1.0 / 3.0]])
    line_inverse = np.array([[4.0, -2.0], [-2.0, 4.0]])
    line_drift = np.array([[-0.5, -0.5], [0.5, 0.5]])
    basis = triple(linear, linear, linear)
    gradient = np.stack(
        [
            triple(slopes, quadratic, quadratic),
            triple(quadratic, slopes, quadratic),
            triple(quadratic, quadratic, slopes),
        ],
        1,
    ).reshape(8, 81)
    inverse = triple(line_inverse, line_inverse, line_inverse)
    project = inverse @ basis.T / 8.0
    stiffness = np.stack(
        [
            triple(line_drift, line_mass, line_mass),
            triple(line_mass, line_drift, line_mass),
            triple(line_mass, line_mass, line_drift),
        ]
    )
    face_mass = np.kron(line_mass, line_mass)
    return tuple(
        (
            jnp.asarray(entry_table, jnp.float32)
            for entry_table in (basis, gradient, inverse, project, stiffness, face_mass)
        )
    )


def face_weight(fluxes, face_mass):
    layout = fluxes.shape
    grouped = fluxes.reshape(layout[0], 4, -1)
    return jnp.einsum("ab,fbn->fan", face_mass, grouped, precision=highest).reshape(layout)


def upwind(left_trace, right_trace, speeds, face_mass):
    fluxes = 0.5 * speeds * (left_trace + right_trace) + 0.5 * jnp.abs(speeds) * (
        left_trace - right_trace
    )
    return face_weight(fluxes, face_mass)


def lagrange_section(conserved, velocity, tables):
    basis, gradient, inverse, project, stiffness, face_mass = tables
    layout = conserved.shape
    zone_count = layout[4] * layout[5] * layout[6]
    fields = conserved.reshape(2, 8, zone_count)
    node_motion = velocity.reshape(81, zone_count)
    divergence = jnp.dot(gradient, node_motion, precision=highest)
    pressure = gamma_less * jnp.dot(basis, fields[1], precision=highest)
    energy = fields[1] - force_step * jnp.dot(project, pressure * divergence, precision=highest)
    lagrange = jnp.stack([fields[0], energy]).reshape(layout)
    mean_motion = jnp.sum(velocity.reshape(3, 27, layout[4], layout[5], layout[6]), axis=1) / 27.0
    padded = jnp.pad(mean_motion, ((0, 0), (0, 0), (0, 0), (1, 1)))
    relaxed = 0.25 * (padded[..., :-2] + 2.0 * mean_motion + padded[..., 2:])
    return (lagrange, mean_motion - relaxed)


def advect(lagrange, relative, x_faces, y_faces, tables):
    basis, gradient, inverse, project, stiffness, face_mass = tables
    layout = lagrange.shape
    zone_count = layout[4] * layout[5] * layout[6]
    flat_state = lagrange.reshape(2, 8, zone_count)
    volume = jnp.zeros_like(flat_state)
    for direction in range(3):
        volume = volume + jnp.einsum(
            "jk,fkn->fjn", stiffness[direction], flat_state, precision=highest
        ) * relative[direction].reshape(1, 1, zone_count)
    padded_z = jnp.pad(lagrange, ((0, 0),) * 6 + ((1, 1),))
    motion_z = jnp.pad(relative[2], ((0, 0), (0, 0), (1, 1)))
    flux_z = upwind(
        padded_z[:, :, :, 1, :, :, :-1],
        padded_z[:, :, :, 0, :, :, 1:],
        0.5 * (motion_z[..., :-1] + motion_z[..., 1:]),
        face_mass,
    )
    face_z = jnp.stack([-flux_z[..., :-1], flux_z[..., 1:]], axis=3)
    flux_x = upwind(x_faces[0], x_faces[1], x_faces[2], face_mass)
    face_x = jnp.stack([-flux_x[:, :, :, :-1], flux_x[:, :, :, 1:]], axis=1)
    flux_y = upwind(y_faces[0], y_faces[1], y_faces[2], face_mass)
    face_y = jnp.stack([-flux_y[:, :, :, :, :-1], flux_y[:, :, :, :, 1:]], axis=2)
    balance = volume - (face_x + face_y + face_z).reshape(2, 8, zone_count)
    remapped = flat_state + advect_step * jnp.einsum(
        "jk,fkn->fjn", inverse, balance, precision=highest
    )
    return remapped.reshape(layout)


def body(conserved, velocity, targets, handoff_blocks, handoff_owner):
    tables = build_tables()
    lagrange, relative = lagrange_section(conserved, velocity, tables)
    width_x = lagrange.shape[4]
    width_y = lagrange.shape[5]
    depth_z = lagrange.shape[6]
    count_px = lax.axis_size("px")
    count_py = lax.axis_size("py")
    total_zones = 8.0 * width_x * width_y * depth_z * count_px * count_py
    upper_x = jnp.concatenate(
        [lagrange[:, 1, :, :, -1].reshape((8, width_y, depth_z)), relative[0, -1][None]], axis=0
    )
    lower_x = jnp.concatenate(
        [lagrange[:, 0, :, :, 0].reshape((8, width_y, depth_z)), relative[0, 0][None]], axis=0
    )
    below_x = passed_along(upper_x, "px", 1)
    above_x = passed_along(lower_x, "px", -1)
    left_x = jnp.concatenate(
        [below_x[:8].reshape((2, 2, 2, 1, width_y, depth_z)), lagrange[:, 1]], axis=3
    )
    right_x = jnp.concatenate(
        [lagrange[:, 0], above_x[:8].reshape((2, 2, 2, 1, width_y, depth_z))], axis=3
    )
    motion_x = jnp.concatenate([below_x[8][None], relative[0], above_x[8][None]], axis=0)
    x_faces = (left_x, right_x, 0.5 * (motion_x[:-1] + motion_x[1:]))
    upper_y = jnp.concatenate(
        [lagrange[:, :, 1, :, :, -1].reshape((8, width_x, depth_z)), relative[1][:, -1][None]],
        axis=0,
    )
    lower_y = jnp.concatenate(
        [lagrange[:, :, 0, :, :, 0].reshape((8, width_x, depth_z)), relative[1][:, 0][None]], axis=0
    )
    below_y = passed_along(upper_y, "py", 1)
    above_y = passed_along(lower_y, "py", -1)
    left_y = jnp.concatenate(
        [below_y[:8].reshape((2, 2, 2, width_x, 1, depth_z)), lagrange[:, :, 1]], axis=4
    )
    right_y = jnp.concatenate(
        [lagrange[:, :, 0], above_y[:8].reshape((2, 2, 2, width_x, 1, depth_z))], axis=4
    )
    motion_y = jnp.concatenate([below_y[8][:, None], relative[1], above_y[8][:, None]], axis=1)
    y_faces = (left_y, right_y, 0.5 * (motion_y[:, :-1] + motion_y[:, 1:]))
    remapped = advect(lagrange, relative, x_faces, y_faces, tables)
    totals = lax.psum(jnp.sum(remapped.reshape(2, -1), axis=1), ("px", "py"))
    field_means = totals / total_zones
    fixed_state = remapped * (targets / field_means).reshape(2, 1, 1, 1, 1, 1, 1)
    entries = handoff_blocks.shape[1]
    capacity = max(2, 2 * entries // count_py)
    blocks = handoff_blocks[0]
    owners = handoff_owner[0, :, 0]
    onehot = (owners[:, None] == jnp.arange(count_py, dtype=jnp.int32)).astype(jnp.int32)
    earlier = jnp.cumsum(onehot, axis=0) - onehot
    slot_index = jnp.sum(onehot * earlier, axis=1)
    position = owners * capacity + slot_index
    placing = (
        position[None, :] == jnp.arange(count_py * capacity, dtype=jnp.int32)[:, None]
    ).astype(jnp.float32)
    columns = fixed_state.reshape((16, width_x * width_y, depth_z))
    picked = jnp.take(columns, blocks, axis=1)
    send_rows = jnp.einsum("sn,cnz->scz", placing, picked, precision=highest).reshape(
        (count_py, capacity, 16, depth_z)
    )
    received = lax.all_to_all(send_rows, "py", split_axis=0, concat_axis=0, tiled=True)
    handed = received.reshape((1, count_py * capacity, 16, depth_z))
    return (fixed_state, handed)


def solution(mesh):
    return jax.shard_map(
        body,
        mesh=mesh,
        in_specs=(
            P(None, None, None, None, "px", "py", None),
            P(None, None, None, None, "px", "py", None),
            P(),
            P("px", "py"),
            P("px", "py", None),
        ),
        out_specs=(P(None, None, None, None, "px", "py", None), P("px", "py", None, None)),
        check_vma=False,
    )
```

profile of v0, /device:TPU:0, one launch (start us, length us, event | category | flops | bytes accessed | tf_op | source)
XLA Modules:
  0.0 75.8 jit_solution(11837693475548157601)
XLA Ops:
  0.6 1.0 %fusion.62 = (f32[1,2,2,2,4,8,128]{6,5,4,3,2,1,0:T(8,128)S(1)}, f32[1,2,2,2,4,8,128]{6,5,4,3,2,1,0:T(8,128)S(1)}) fusion(f32[2,2,2,2,4,8,128]{6,5,4,3,2,1,0:T(8,128)} %param.11), kind=kLoop, calls=%fused_computation.139 | loop fusion | bytes 524288 | tf_op jit(solution)/shard_map/slice | solution.py:91
  1.7 1.5 %reshape.163 = f32[81,4096]{1,0:T(8,128)S(1)} reshape(f32[3,3,3,3,4,8,128]{6,5,4,3,2,1,0:T(8,128)} %param.12) | data formatting | bytes 2654208 | tf_op jit(solution)/shard_map/reshape | solution.py:88
  3.3 0.3 convolution_multiply_fusion.6
  3.5 0.8 %convolution_multiply_fusion.5 = f32[8,4096]{1,0:T(8,128)S(1)} fusion(f32[8,4096]{1,0:T(8,128)S(1)} %convolution_multiply_fusion.6, f32[8,81]{1,0:T(8,128)S(1)} %copy-done.8, f32[81,4096]{1,0:T(8,128)S(1)} %reshape.163), kind=kOutput, calls=%fused_computation.17 | convolution fusion | flops 31883264 | bytes 1591840 | tf_op jit(solution)/shard_map/dot_general | solution.py:89
  4.3 0.3 fusion.7
  4.9 2.4 %collective-permute-start.2 = (f32[9,4,128]{2,1,0:T(4,128)S(1)}, f32[9,4,128]{2,1,0:T(4,128)S(1)}, u32[]{:S(2)}, u32[]{:S(2)}) collective-permute-start(f32[9,4,128]{2,1,0:T(4,128)S(1)} %pad_maximum_fusion.11), channel_id=1, source_target_pairs={{0,1},{1,2},{2,3},{4,5},{5,6},{6,7},{8,9},{9,10},{10,11},{12,13},{... | collective-permute-start | bytes 55304 | tf_op jit(solution)/shard_map/ppermute | solution.py:18
  7.4 1.3 %collective-permute-start.3 = (f32[9,4,128]{2,1,0:T(4,128)S(1)}, f32[9,4,128]{2,1,0:T(4,128)S(1)}, u32[]{:S(2)}, u32[]{:S(2)}) collective-permute-start(f32[9,4,128]{2,1,0:T(4,128)S(1)} %pad_maximum_fusion.12), channel_id=1, source_target_pairs={{1,0},{2,1},{3,2},{5,4},{6,5},{7,6},{9,8},{10,9},{11,10},{13,12},{... | collective-permute-start | bytes 55304 | tf_op jit(solution)/shard_map/ppermute | solution.py:18
  8.7 4.2 %collective-permute-start = (f32[9,8,128]{2,1,0:T(8,128)S(1)}, f32[9,8,128]{2,1,0:T(8,128)S(1)}, u32[]{:S(2)}, u32[]{:S(2)}) collective-permute-start(f32[9,8,128]{2,1,0:T(8,128)S(1)} %pad_maximum_fusion.9), channel_id=1, source_target_pairs={{0,4},{4,8},{8,12},{12,16},{16,20},{20,24},{24,28},{1,5},{5,9},{9,... | collective-permute-start | bytes 110600 | tf_op jit(solution)/shard_map/ppermute | solution.py:18
  12.9 1.3 %collective-permute-start.1 = (f32[9,8,128]{2,1,0:T(8,128)S(1)}, f32[9,8,128]{2,1,0:T(8,128)S(1)}, u32[]{:S(2)}, u32[]{:S(2)}) collective-permute-start(f32[9,8,128]{2,1,0:T(8,128)S(1)} %pad_maximum_fusion.10), channel_id=1, source_target_pairs={{4,0},{8,4},{12,8},{16,12},{20,16},{24,20},{28,24},{5,1},{9,5},{13... | collective-permute-start | bytes 110600 | tf_op jit(solution)/shard_map/ppermute | solution.py:18
  14.4 0.2 fusion.12
  14.6 0.2 add.125
  14.9 0.2 sub.40
  15.5 0.4 convolution_bitcast_fusion
  15.9 0.3 reshape.170
  16.3 0.2 reduce_window_sum.11
  16.5 0.3 convolution_multiply_fusion.3
  16.9 0.4 fusion.5
  17.6 0.4 convolution_bitcast_fusion.1
  18.2 0.6 collective-permute-done.1
  19.0 0.4 convolution_bitcast_fusion.2
  19.8 0.5 copy-done.3
  20.2 0.4 fusion.4
  20.6 0.4 fusion.65
  21.1 43.9 %psum.7 = f32[2]{0:T(128)S(1)} all-reduce(f32[2]{0:T(128)S(1)} %get-tuple-element.40), channel_id=1, replica_groups=mesh['px'=8,'py'=4] {'px','py'}, use_global_device_ids=true, to_apply=%region_2.3 | all-reduce | flops 2 | bytes 16 | tf_op jit(solution)/shard_map/psum | solution.py:172
  65.2 0.2 copy_multiply_fusion
  65.4 0.6 gather_fusion
  66.0 0.3 fusion.41
  66.4 0.7 copy.106
  67.0 3.5 %all-to-all-start = ((f32[4,4,16,128]{3,1,2,0:T(4,128)}), f32[4,4,16,128]{3,1,2,0:T(4,128)S(1)}, u32[]{:S(2)}, u32[]{:S(2)}) async-start(f32[4,4,16,128]{3,1,2,0:T(4,128)} %copy.106), calls=%async_computation | async-start | bytes 262144 | tf_op jit(solution)/shard_map/all_to_all | solution.py:191
  70.6 0.8 %broadcast_multiply_fusion = f32[2,2,2,2,4,8,128]{6,5,4,3,2,1,0:T(8,128)} fusion(f32[2,2,2,2,4,8,128]{6,5,4,3,2,1,0:T(8,128)S(1)} %bitcast.158, f32[2]{0:T(128)S(1)} %multiply_divide_fusion), kind=kLoop, calls=%fused_computation.78 | loop fusion | flops 65536 | bytes 524296 | tf_op jit(solution)/shard_map/mul | solution.py:174
  71.4 3.8 %all-to-all-done = f32[4,4,16,128]{3,1,2,0:T(4,128)S(1)} async-done(((f32[4,4,16,128]{3,1,2,0:T(4,128)}), f32[4,4,16,128]{3,1,2,0:T(4,128)S(1)}, u32[]{:S(2)}, u32[]{:S(2)}) %all-to-all-start) | async-done | bytes 131104 | tf_op jit(solution)/shard_map/all_to_all | solution.py:191
  75.2 0.7 copy.107
  (86 shorter events, 2.0 us)
Async XLA Ops:
  1.7 1.6 %copy-start.6 = (f32[8,8]{1,0:T(8,128)S(1)}, f32[8,8]{1,0:T(8,128)}, u32[]{:S(2)}) copy-start(f32[8,8]{1,0:T(8,128)} %constant.61.clone) | copy-start | bytes 772
  1.7 1.9 %copy-start.8 = (f32[8,81]{1,0:T(8,128)S(1)}, f32[8,81]{1,0:T(8,128)}, u32[]{:S(2)}) copy-start(f32[8,81]{1,0:T(8,128)} %constant.62.clone) | copy-start | bytes 7780
  3.2 1.1 %copy-start.7 = (f32[8,8]{1,0:T(8,128)S(1)}, f32[8,8]{1,0:T(8,128)}, u32[]{:S(2)}) copy-start(f32[8,8]{1,0:T(8,128)} %constant.64.clone) | copy-start | bytes 772
  3.3 1.4 %copy-start = (f32[3,3,3,3,4,8,128]{6,5,4,3,2,1,0:T(8,128)S(1)}, f32[3,3,3,3,4,8,128]{6,5,4,3,2,1,0:T(8,128)}, u32[]{:S(2)}) copy-start(f32[3,3,3,3,4,8,128]{6,5,4,3,2,1,0:T(8,128)} %param.12) | copy-start | bytes 3981316
  4.8 9.5 %copy-start.10 = (s32[1,8]{1,0:T(1,128)S(1)}, s32[1,8]{1,0:T(1,128)}, u32[]{:S(2)}) copy-start(s32[1,8]{1,0:T(1,128)} %param.14) | copy-start | bytes 100
  4.9 12.3 %collective-permute-start.2 = (f32[9,4,128]{2,1,0:T(4,128)S(1)}, f32[9,4,128]{2,1,0:T(4,128)S(1)}, u32[]{:S(2)}, u32[]{:S(2)}) collective-permute-start(f32[9,4,128]{2,1,0:T(4,128)S(1)} %pad_maximum_fusion.11), channel_id=1, source_target_pairs={{0,1},{1,2},{2,3},{4,5},{5,6},{6,7},{8,9},{9,10},{10,11},{12,13},{... | collective-permute-start | bytes 55304 | tf_op jit(solution)/shard_map/ppermute | solution.py:18
  7.4 9.9 %collective-permute-start.3 = (f32[9,4,128]{2,1,0:T(4,128)S(1)}, f32[9,4,128]{2,1,0:T(4,128)S(1)}, u32[]{:S(2)}, u32[]{:S(2)}) collective-permute-start(f32[9,4,128]{2,1,0:T(4,128)S(1)} %pad_maximum_fusion.12), channel_id=1, source_target_pairs={{1,0},{2,1},{3,2},{5,4},{6,5},{7,6},{9,8},{10,9},{11,10},{13,12},{... | collective-permute-start | bytes 55304 | tf_op jit(solution)/shard_map/ppermute | solution.py:18
  8.7 9.4 %collective-permute-start = (f32[9,8,128]{2,1,0:T(8,128)S(1)}, f32[9,8,128]{2,1,0:T(8,128)S(1)}, u32[]{:S(2)}, u32[]{:S(2)}) collective-permute-start(f32[9,8,128]{2,1,0:T(8,128)S(1)} %pad_maximum_fusion.9), channel_id=1, source_target_pairs={{0,4},{4,8},{8,12},{12,16},{16,20},{20,24},{24,28},{1,5},{5,9},{9,... | collective-permute-start | bytes 110600 | tf_op jit(solution)/shard_map/ppermute | solution.py:18
  12.9 5.9 %collective-permute-start.1 = (f32[9,8,128]{2,1,0:T(8,128)S(1)}, f32[9,8,128]{2,1,0:T(8,128)S(1)}, u32[]{:S(2)}, u32[]{:S(2)}) collective-permute-start(f32[9,8,128]{2,1,0:T(8,128)S(1)} %pad_maximum_fusion.10), channel_id=1, source_target_pairs={{4,0},{8,4},{12,8},{16,12},{20,16},{24,20},{28,24},{5,1},{9,5},{13... | collective-permute-start | bytes 110600 | tf_op jit(solution)/shard_map/ppermute | solution.py:18
  14.3 1.2 %copy-start.1 = (f32[4,4,1]{1,0,2:T(4,128)S(1)}, f32[4,4,1]{1,0,2:T(4,128)}, u32[]{:S(2)}) copy-start(f32[4,4,1]{1,0,2:T(4,128)} %constant.86) | copy-start | bytes 196
  14.4 1.9 %copy-start.9 = (s32[1,8,1]{1,2,0:T(1,128)S(1)}, s32[1,8,1]{1,2,0:T(1,128)}, u32[]{:S(2)}) copy-start(s32[1,8,1]{1,2,0:T(1,128)} %param.15) | copy-start | bytes 100
  14.6 1.9 %copy-start.5 = (f32[8,8,1]{1,0,2:T(8,128)S(1)}, f32[8,8,1]{1,0,2:T(8,128)}, u32[]{:S(2)}) copy-start(f32[8,8,1]{1,0,2:T(8,128)} %constant.83) | copy-start | bytes 772
  14.9 2.0 %copy-start.4 = (f32[8,8,1]{1,0,2:T(8,128)S(1)}, f32[8,8,1]{1,0,2:T(8,128)}, u32[]{:S(2)}) copy-start(f32[8,8,1]{1,0,2:T(8,128)} %constant.84) | copy-start | bytes 772
  19.5 0.7 copy-start.3
  19.6 1.0 %copy-start.2 = (f32[8,8,1]{1,0,2:T(8,128)S(1)}, f32[8,8,1]{1,0,2:T(8,128)}, u32[]{:S(2)}) copy-start(f32[8,8,1]{1,0,2:T(8,128)} %constant.87) | copy-start | bytes 772
  19.7 45.4 %copy-start.11 = (f32[2]{0:T(128)S(1)}, f32[2]{0:T(128)}, u32[]{:S(2)}) copy-start(f32[2]{0:T(128)} %param.13) | copy-start | bytes 28
  67.0 8.1 %all-to-all-start = ((f32[4,4,16,128]{3,1,2,0:T(4,128)}), f32[4,4,16,128]{3,1,2,0:T(4,128)S(1)}, u32[]{:S(2)}, u32[]{:S(2)}) async-start(f32[4,4,16,128]{3,1,2,0:T(4,128)} %copy.106), calls=%async_computation | async-start | bytes 262144 | tf_op jit(solution)/shard_map/all_to_all | solution.py:191
where the time goes:
time: 76.3 us; the launch traced here: 75.8 us
  blocking collectives  43.9 us (58%)
  starting transfers between devices  12.7 us (17%)
  local copies, waits for them, and re-layouts  6.92 us (9%)
  waiting for transfers between devices  4.44 us (6%)
  matrix products  4.35 us (6%)
  other arithmetic  2.08 us (3%)
  between operations  1.39 us (2%)
    psum x1, blocking collectives, body(): totals = lax.psum(jnp.sum(remapped.reshape(2, -1), axis=1), ('px', 'py'))  43.9 us
    ppermute x4, starting transfers between devices, passed_along(): return lax.ppermute(x, axis, pairs)  9.2 us
    all_to_all x1, waiting for transfers between devices, body(): lax.all_to_all(send_rows, 'py', split_axis=0, concat_axis=0, tiled=True)  3.81 us
    all_to_all x1, starting transfers between devices, body(): lax.all_to_all(send_rows, 'py', split_axis=0, concat_axis=0, tiled=True)  3.54 us
    reshape x1, local copies, waits for them, and re-layouts, lagrange_section(): node_motion = velocity.reshape(81, zone_count)  1.54 us
  transfers between devices with their start and end apart: 5, of which 2 were waited for; matrix products, arithmetic and copies ran while one was open for 6% of the time, Pallas kernels for 0%

commit v1 on v0

v1 whole, which is shorter than its diff:
```python
import functools
import math

import jax
import jax.numpy as jnp
from jax import lax
from jax.experimental import pallas as pl
from jax.experimental.pallas import tpu as pltpu
from jax.sharding import PartitionSpec as P

gamma_less = 0.4
force_step = 0.02
gauss_offset = 0.5 / math.sqrt(3.0)


def in_vmem():
    return pl.BlockSpec(memory_space=pltpu.VMEM)


def in_place():
    return pl.BlockSpec(memory_space=pl.ANY)


def shape_of(*shape):
    return jax.ShapeDtypeStruct(shape, jnp.float32)


def kernel_options():
    return pltpu.CompilerParams(vmem_limit_bytes=16 * 1024 * 1024)


def paired(size, first):
    pairs = []
    for low in range(first, size - 1, 2):
        pairs += [(low, low + 1), (low + 1, low)]
    return pairs


def partner_of(index, hop, size):
    if size & (size - 1) == 0:
        return index ^ hop
    return lax.rem(index + hop, size)


def giver_of(index, hop, size):
    if size & (size - 1) == 0:
        return index ^ hop
    return lax.rem(index + size - hop, size)


def lifted(low, high, value):
    middle = 0.5 * (low + high)
    tilt = value * (low - high)
    return middle + tilt, middle - tilt


def along(values, direction, operation):
    stride = (4, 2, 1)[direction]
    out = [None] * 8
    for low in range(8):
        if not low & stride:
            out[low], out[low + stride] = operation(values[low], values[low + stride])
    return out


def quadratic_values(first, second, third):
    middle = (1.0 / 6.0) * (first + third) + (2.0 / 3.0) * second
    tilt = gauss_offset * (third - first)
    return middle - tilt, middle + tilt


def quadratic_slopes(first, second, third):
    rise = third - first
    bend = (4.0 * gauss_offset) * ((first + third) - 2.0 * second)
    return rise - bend, rise + bend


def lagrange_kernel(
    sizes,
    conserved_ref,
    velocity_ref,
    state_ref,
    relative_ref,
    xa_ref,
    xb_ref,
    ya_ref,
    yb_ref,
    motion_ref,
    state_sem,
    motion_sem,
):
    width_x, width_y, depth_z = sizes
    copies = []
    for x in range(width_x):
        copies.append(
            (
                pltpu.make_async_copy(
                    conserved_ref.at[:, x], state_ref.at[:, x], state_sem.at[x]
                ),
                pltpu.make_async_copy(
                    velocity_ref.at[:, x], motion_ref.at[:, x], motion_sem.at[x]
                ),
            )
        )
    for state_copy, motion_copy in copies:
        state_copy.start()
        motion_copy.start()
    lane = lax.broadcasted_iota(jnp.int32, (width_y, depth_z), 1)
    for x in range(width_x):
        copies[x][0].wait()
        copies[x][1].wait()
        divergence = [None] * 8
        for component in range(3):

            def node(a, b, c):
                return motion_ref[component * 27 + a * 9 + b * 3 + c, x]

            total = None
            stage = {}
            for a in range(3):
                for b in range(3):
                    line = [node(a, b, c) for c in range(3)]
                    part = (line[0] + line[1]) + line[2]
                    total = part if total is None else total + part
                    rule = quadratic_slopes if component == 2 else quadratic_values
                    stage[a, b, 0], stage[a, b, 1] = rule(*line)
            second = {}
            for a in range(3):
                for c in range(2):
                    rule = quadratic_slopes if component == 1 else quadratic_values
                    second[a, 0, c], second[a, 1, c] = rule(
                        stage[a, 0, c], stage[a, 1, c], stage[a, 2, c]
                    )
            for b in range(2):
                for c in range(2):
                    rule = quadratic_slopes if component == 0 else quadratic_values
                    pair = rule(second[0, b, c], second[1, b, c], second[2, b, c])
                    for a in range(2):
                        point = a * 4 + b * 2 + c
                        divergence[point] = (
                            pair[a] if component == 0 else divergence[point] + pair[a]
                        )
            mean = total * (1.0 / 27.0)
            before = jnp.where(lane == 0, 0.0, pltpu.roll(mean, 1, 1))
            after = jnp.where(lane == depth_z - 1, 0.0, pltpu.roll(mean, depth_z - 1, 1))
            relative_ref[component, x] = mean - 0.25 * ((before + 2.0 * mean) + after)
        energy = [state_ref[8 + corner, x] for corner in range(8)]
        work = energy
        for direction in range(3):
            work = along(work, direction, lambda p, q: lifted(p, q, gauss_offset))
        work = [(gamma_less * work[point]) * divergence[point] for point in range(8)]
        for direction in range(3):
            work = along(work, direction, lambda p, q: lifted(p, q, 3.0 * gauss_offset))
        for corner in range(8):
            state_ref[8 + corner, x] = energy[corner] - force_step * work[corner]
    odd_x = lax.rem(lax.axis_index("px"), 2)
    for out_ref, side in ((xa_ref, 1 - odd_x), (xb_ref, odd_x)):
        place = side * (width_x - 1)
        for field in range(2):
            for k in range(4):
                out_ref[field * 4 + k] = state_ref[field * 8 + side * 4 + k, place]
        out_ref[8] = relative_ref[0, place]
    odd_y = lax.rem(lax.axis_index("py"), 2)
    state_rows = state_ref.reshape(16 * width_x * width_y, depth_z)
    relative_rows = relative_ref.reshape(3 * width_x * width_y, depth_z)
    column = width_x * width_y
    for out_ref, side in ((ya_ref, 1 - odd_y), (yb_ref, odd_y)):
        place = side * (width_y - 1)
        for field in range(2):
            for a in range(2):
                for c in range(2):
                    start = (field * 8 + a * 4 + c) * column + side * 2 * column + place
                    out_ref[field * 4 + a * 2 + c] = state_rows[
                        pl.ds(start, width_x, stride=width_y), :
                    ]
        out_ref[8] = relative_rows[pl.ds(column + place, width_x, stride=width_y), :]


def lagrange_call(conserved, velocity):
    width_x, width_y, depth_z = conserved.shape[4:]
    sizes = (width_x, width_y, depth_z)
    return pl.pallas_call(
        functools.partial(lagrange_kernel, sizes),
        out_shape=(
            shape_of(16, *sizes),
            shape_of(3, *sizes),
            shape_of(9, width_y, depth_z),
            shape_of(9, width_y, depth_z),
            shape_of(9, width_x, depth_z),
            shape_of(9, width_x, depth_z),
        ),
        in_specs=[in_place()] * 2,
        out_specs=(in_vmem(),) * 6,
        scratch_shapes=[
            pltpu.VMEM((81,) + sizes, jnp.float32),
            pltpu.SemaphoreType.DMA((width_x,)),
            pltpu.SemaphoreType.DMA((width_x,)),
        ],
        compiler_params=kernel_options(),
        name="lagrange",
    )(conserved.reshape((16,) + sizes), velocity.reshape((81,) + sizes))


def remap_kernel(
    sizes,
    count_py,
    entries,
    capacity,
    state_ref,
    relative_ref,
    xa_ref,
    xb_ref,
    ya_ref,
    yb_ref,
    blocks_hbm,
    owners_hbm,
    targets_hbm,
    *refs,
):
    width_x, width_y, depth_z = sizes
    out_ref, total_ref, goal_ref = refs[:3]
    send_refs = refs[3 : 3 + count_py]
    sending, blocks_ref, owners_ref, targets_ref, sems = refs[3 + count_py :]
    copies = [
        pltpu.make_async_copy(blocks_hbm, blocks_ref, sems.at[0]),
        pltpu.make_async_copy(owners_hbm, owners_ref, sems.at[1]),
        pltpu.make_async_copy(targets_hbm, targets_ref, sems.at[2]),
    ]
    for copy in copies:
        copy.start()
    lane = lax.broadcasted_iota(jnp.int32, (width_y, depth_z), 1)
    row = lax.broadcasted_iota(jnp.int32, (width_y, depth_z), 0)
    even_x = lax.rem(lax.axis_index("px"), 2) == 0
    even_y = lax.rem(lax.axis_index("py"), 2) == 0

    def below_x(k):
        return jnp.where(even_x, xb_ref[k], xa_ref[k])

    def above_x(k):
        return jnp.where(even_x, xa_ref[k], xb_ref[k])

    def split(speed):
        return jnp.maximum(speed, 0.0), jnp.minimum(speed, 0.0)

    sending[...] = jnp.zeros(sending.shape, jnp.float32)
    totals = [None, None]
    speed = relative_ref[0, 0]
    coefficient = split(0.5 * (below_x(8) + speed))
    lower_x = [
        coefficient[0] * below_x(field * 4 + k) + coefficient[1] * state_ref[field * 8 + k, 0]
        for field in range(2)
        for k in range(4)
    ]
    for x in range(width_x):
        speed_x, speed_y, speed_z = (relative_ref[d, x] for d in range(3))
        beyond = above_x(8) if x == width_x - 1 else relative_ref[0, x + 1]
        upper_x_rate = split(0.5 * (speed_x + beyond))
        y_below = jnp.where(even_y, yb_ref[8, pl.ds(x, 1), :], ya_ref[8, pl.ds(x, 1), :])
        y_above = jnp.where(even_y, ya_ref[8, pl.ds(x, 1), :], yb_ref[8, pl.ds(x, 1), :])
        lower_y_rate = split(
            0.5 * (jnp.where(row == 0, y_below, pltpu.roll(speed_y, 1, 0)) + speed_y)
        )
        upper_y_rate = split(
            0.5
            * (
                speed_y
                + jnp.where(row == width_y - 1, y_above, pltpu.roll(speed_y, width_y - 1, 0))
            )
        )
        first = lane == 0
        last = lane == depth_z - 1
        rate = split(0.5 * (jnp.where(first, 0.0, pltpu.roll(speed_z, 1, 1)) + speed_z))
        lower_z_rate = (jnp.where(first, 0.0, rate[0]), rate[1])
        rate = split(
            0.5 * (speed_z + jnp.where(last, 0.0, pltpu.roll(speed_z, depth_z - 1, 1)))
        )
        upper_z_rate = (rate[0], jnp.where(last, 0.0, rate[1]))
        drift = (1.5 * speed_x, 1.5 * speed_y, 1.5 * speed_z)
        upper_x = []
        for field in range(2):
            state = [state_ref[field * 8 + corner, x] for corner in range(8)]
            result = list(state)

            def update(low, high, low_flux, high_flux, d):
                both = low_flux + high_flux
                flow = drift[d] * (state[low] + state[high])
                result[low] = result[low] + ((both + low_flux) - flow)
                result[high] = result[high] + (flow - (both + high_flux))

            for k in range(4):
                low, high = k, k + 4
                across = (
                    above_x(field * 4 + k)
                    if x == width_x - 1
                    else state_ref[field * 8 + k, x + 1]
                )
                flux = upper_x_rate[0] * state[high] + upper_x_rate[1] * across
                upper_x.append(flux)
                update(low, high, lower_x[field * 4 + k], flux, 0)
            for a in range(2):
                for c in range(2):
                    low = a * 4 + c
                    high = low + 2
                    k = field * 4 + a * 2 + c
                    ya = ya_ref[k, pl.ds(x, 1), :]
                    yb = yb_ref[k, pl.ds(x, 1), :]
                    left = jnp.where(
                        row == 0, jnp.where(even_y, yb, ya), pltpu.roll(state[high], 1, 0)
                    )
                    right = jnp.where(
                        row == width_y - 1,
                        jnp.where(even_y, ya, yb),
                        pltpu.roll(state[low], width_y - 1, 0),
                    )
                    update(
                        low,
                        high,
                        lower_y_rate[0] * left + lower_y_rate[1] * state[low],
                        upper_y_rate[0] * state[high] + upper_y_rate[1] * right,
                        1,
                    )
            for k in range(4):
                low, high = 2 * k, 2 * k + 1
                left = pltpu.roll(state[high], 1, 1)
                right = pltpu.roll(state[low], depth_z - 1, 1)
                update(
                    low,
                    high,
                    lower_z_rate[0] * left + lower_z_rate[1] * state[low],
                    upper_z_rate[0] * state[high] + upper_z_rate[1] * right,
                    2,
                )
            part = None
            for corner in range(8):
                out_ref[field * 8 + corner, x] = result[corner]
                part = result[corner] if part is None else part + result[corner]
            totals[field] = part if totals[field] is None else totals[field] + part
        lower_x = upper_x
    total_ref[...] = jnp.broadcast_to(folded(totals)[None], total_ref.shape)
    for copy in copies:
        copy.wait()
    half = lax.broadcasted_iota(jnp.int32, goal_ref.shape, 1) < depth_z // 2
    goal_ref[...] = jnp.where(half, targets_ref[0], targets_ref[1])
    place = lax.axis_index("py")
    rows = out_ref.reshape(16 * width_x * width_y, depth_z)
    owners = [owners_ref[0, entry, 0] for entry in range(entries)]
    for entry in range(entries):
        slot = jnp.int32(0)
        for earlier in range(entry):
            slot = slot + jnp.where(owners[earlier] == owners[entry], 1, 0)
        if count_py & (count_py - 1) == 0:
            hop = owners[entry] ^ place
        else:
            hop = lax.rem(owners[entry] - place + count_py, count_py)
        sending[hop * capacity + slot] = rows[
            pl.ds(blocks_ref[0, entry], 16, stride=width_x * width_y), :
        ]
    for hop in range(count_py):
        send_refs[hop][...] = sending[pl.ds(hop * capacity, capacity)]


def folded(totals):
    rows = [jnp.sum(total, axis=0, keepdims=True) for total in totals]
    depth = rows[0].shape[1]
    rows = [row + pltpu.roll(row, depth // 2, 1) for row in rows]
    half = lax.broadcasted_iota(jnp.int32, rows[0].shape, 1) < depth // 2
    return jnp.where(half, rows[0], rows[1])


def remap_call(state, relative, halos, blocks, owners, targets, device_count, count_py):
    sizes = state.shape[1:]
    width_x, width_y, depth_z = sizes
    entries = blocks.shape[1]
    capacity = max(2, 2 * entries // count_py)
    return pl.pallas_call(
        functools.partial(remap_kernel, sizes, count_py, entries, capacity),
        out_shape=(
            shape_of(16, *sizes),
            shape_of(device_count, 1, depth_z),
            shape_of(1, depth_z),
        )
        + (shape_of(capacity, 16, depth_z),) * count_py,
        in_specs=[in_vmem()] * 6 + [in_place()] * 3,
        out_specs=(in_vmem(),) * (3 + count_py),
        scratch_shapes=[
            pltpu.VMEM((count_py * capacity, 16, depth_z), jnp.float32),
            pltpu.SMEM(blocks.shape, jnp.int32),
            pltpu.SMEM(owners.shape, jnp.int32),
            pltpu.SMEM(targets.shape, jnp.float32),
            pltpu.SemaphoreType.DMA((3,)),
        ],
        compiler_params=kernel_options(),
        name="remap",
    )(state, relative, *halos, blocks, owners, targets)


def scale_kernel(total_nodes, state_ref, total_ref, goal_ref, fixed_ref, scale_ref):
    total = jnp.sum(total_ref[...], axis=0)
    half = lax.broadcasted_iota(jnp.int32, total.shape, 1) < total.shape[1] // 2
    sums = (
        jnp.sum(jnp.where(half, total, 0.0), axis=1, keepdims=True),
        jnp.sum(jnp.where(half, 0.0, total), axis=1, keepdims=True),
    )
    means = jnp.where(half, sums[0], sums[1]) / total_nodes
    scale = goal_ref[...] / means
    other = pltpu.roll(scale, scale.shape[1] // 2, 1)
    factors = (jnp.where(half, scale, other), jnp.where(half, other, scale))
    for field in range(2):
        scale_ref[pl.ds(field, 1), :] = factors[field]
        fixed_ref[pl.ds(field * 8, 8)] = state_ref[pl.ds(field * 8, 8)] * factors[field]


def scale_call(state, gathered, goal, total_nodes):
    return pl.pallas_call(
        functools.partial(scale_kernel, total_nodes),
        out_shape=(shape_of(*state.shape), shape_of(2, state.shape[-1])),
        in_specs=[in_vmem()] * 3,
        out_specs=(in_vmem(),) * 2,
        compiler_params=kernel_options(),
        name="scale",
    )(state, gathered, goal)


def settle_kernel(count_py, capacity, scale_ref, *refs):
    handed_ref = refs[count_py]
    place = lax.axis_index("py")
    for hop in range(count_py):
        start = giver_of(place, hop, count_py) * capacity
        for field in range(2):
            handed_ref[pl.ds(start, capacity), pl.ds(field * 8, 8), :] = (
                refs[hop][:, pl.ds(field * 8, 8), :] * scale_ref[pl.ds(field, 1), :]
            )


def settle_call(scale, chunks):
    count_py = len(chunks)
    capacity = chunks[0].shape[0]
    return pl.pallas_call(
        functools.partial(settle_kernel, count_py, capacity),
        out_shape=shape_of(count_py * capacity, *chunks[0].shape[1:]),
        in_specs=[in_vmem()] * (1 + count_py),
        out_specs=in_vmem(),
        compiler_params=kernel_options(),
        name="settle",
    )(scale, *chunks)


def hop_pairs(size, hop):
    if size & (size - 1) == 0:
        return [(i, i ^ hop) for i in range(size)]
    return [(i, (i + hop) % size) for i in range(size)]


def body(conserved, velocity, targets, handoff_blocks, handoff_owner):
    count_px = lax.axis_size("px")
    count_py = lax.axis_size("py")
    device_count = count_px * count_py
    total_nodes = 8.0 * math.prod(conserved.shape[4:]) * device_count
    state, relative, xa, xb, ya, yb = lagrange_call(conserved, velocity)
    halos = (
        lax.ppermute(xa, "px", paired(count_px, 0)),
        lax.ppermute(xb, "px", paired(count_px, 1)),
        lax.ppermute(ya, "py", paired(count_py, 0)),
        lax.ppermute(yb, "py", paired(count_py, 1)),
    )
    remapped, total, goal, *chunks = remap_call(
        state, relative, halos, handoff_blocks, handoff_owner, targets, device_count, count_py
    )
    received = [chunks[0]] + [
        lax.ppermute(chunks[hop], "py", hop_pairs(count_py, hop)) for hop in range(1, count_py)
    ]
    gathered = lax.all_to_all(total, ("px", "py"), 0, 0, tiled=True)
    fixed, scale = scale_call(remapped, gathered, goal, total_nodes)
    handed = settle_call(scale, received)
    return fixed.reshape(conserved.shape), handed[None]


def solution(mesh):
    return jax.shard_map(
        body,
        mesh=mesh,
        in_specs=(
            P(None, None, None, None, "px", "py", None),
            P(None, None, None, None, "px", "py", None),
            P(),
            P("px", "py"),
            P("px", "py", None),
        ),
        out_specs=(P(None, None, None, None, "px", "py", None), P("px", "py", None, None)),
        check_vma=False,
    )
```

time: 76.3 us -> 32 us (0.42)
  blocking collectives: 43.9 us -> 14.5 us
  local copies, waits for them, and re-layouts: 6.92 us -> 2.38 us
  matrix products: 4.35 us -> 0 us
  waiting for transfers between devices: 4.44 us -> 0.45 us
  Pallas kernels: 0 us -> 3.42 us
  starting transfers between devices: 12.7 us -> 10.3 us
  other arithmetic: 2.08 us -> 0 us
    psum x1 -> x0, blocking collectives: 43.9 us -> none  [body(): totals = lax.psum(jnp.sum(remapped.reshape(2, -1), axis=1), ('px', 'py'))]
    all_to_all x0 -> x1, blocking collectives: none -> 14.5 us  [body(): gathered = lax.all_to_all(total, ('px', 'py'), 0, 0, tiled=True)]
    dot_general x11 -> x0, matrix products: 4.35 us -> none  [the longest x3 1.23 us: face_weight(): jnp.einsum('ab,fbn->fan', face_mass, grouped, precision=highest)]
    all_to_all x1 -> x0, waiting for transfers between devices: 3.81 us -> none  [body(): lax.all_to_all(send_rows, 'py', split_axis=0, concat_axis=0, tiled=True)]
    all_to_all x1 -> x0, starting transfers between devices: 3.54 us -> none  [body(): lax.all_to_all(send_rows, 'py', split_axis=0, concat_axis=0, tiled=True)]
    pallas_call x0 -> x4, Pallas kernels: none -> 3.42 us  [the longest x1 1 us: remap_call(): pl.pallas_call(functools.partial(remap_kernel, sizes, count_py, entries,...]
    reshape x5 -> x0, local copies, waits for them, and re-layouts: 2.69 us -> none  [the longest x1 1.54 us: lagrange_section(): node_motion = velocity.reshape(81, zone_count)]
    unnamed x26 -> x11, local copies, waits for them, and re-layouts: 0.63 us -> 2.38 us
  transfers between devices with their start and end apart: 5 -> 7, of which waited for: 2 -> 1; matrix products, arithmetic and copies ran while one was open for 6% -> 0% of each run, Pallas kernels for 0% -> 3%
where the time goes in v1:
time: 32 us; the launch traced here: 31.8 us
  blocking collectives  14.5 us (45%)
  starting transfers between devices  10.3 us (32%)
  Pallas kernels  3.42 us (11%)
  local copies, waits for them, and re-layouts  2.38 us (7%)
  between operations  0.73 us (2%)
  waiting for transfers between devices  0.45 us (1%)
    all_to_all x1, blocking collectives, body(): gathered = lax.all_to_all(total, ('px', 'py'), 0, 0, tiled=True)  14.5 us
    ppermute x3, starting transfers between devices, body(): lax.ppermute(chunks[hop], 'py', hop_pairs(count_py, hop))  5.87 us
    ppermute x1, starting transfers between devices, body(): lax.ppermute(xa, 'px', paired(count_px, 0))  3.03 us
    unnamed x11, local copies, waits for them, and re-layouts  2.38 us
    pallas_call x1, Pallas kernels, remap_call(): pl.pallas_call(functools.partial(remap_kernel, sizes, count_py, entries,...  1 us
    pallas_call x1, Pallas kernels, scale_call(): pl.pallas_call(functools.partial(scale_kernel, total_nodes), out_shape=(s...  0.91 us
    pallas_call x1, Pallas kernels, lagrange_call(): pl.pallas_call(functools.partial(lagrange_kernel, sizes), out_shape=(shap...  0.84 us
    pallas_call x1, Pallas kernels, settle_call(): pl.pallas_call(functools.partial(settle_kernel, count_py, capacity), out_...  0.67 us
  transfers between devices with their start and end apart: 7, of which 1 were waited for; matrix products, arithmetic and copies ran while one was open for 0% of the time, Pallas kernels for 3%

profile of v1, /device:TPU:0, one launch (start us, length us, event | category | flops | bytes accessed | tf_op | source)
XLA Modules:
  0.0 31.8 jit_solution(6728025631234486984)
XLA Ops:
  0.6 0.0 copy-start.4
  0.6 0.0 copy-start.2
  0.7 0.0 copy-start.3
  0.7 0.0 copy-start
  0.7 1.3 %copy-done = f32[3,3,3,3,4,8,128]{6,5,4,3,2,1,0:T(8,128)S(1)} copy-done((f32[3,3,3,3,4,8,128]{6,5,4,3,2,1,0:T(8,128)S(1)}, f32[3,3,3,3,4,8,128]{6,5,4,3,2,1,0:T(8,128)}, u32[]{:S(2)}) %copy-start) | copy-done | bytes 1327128
  2.0 0.0 copy-start.1
  2.0 0.9 %copy-done.1 = f32[2,2,2,2,4,8,128]{6,5,4,3,2,1,0:T(8,128)S(1)} copy-done((f32[2,2,2,2,4,8,128]{6,5,4,3,2,1,0:T(8,128)S(1)}, f32[2,2,2,2,4,8,128]{6,5,4,3,2,1,0:T(8,128)}, u32[]{:S(2)}) %copy-start.1) | copy-done | bytes 262168
  3.0 0.8 %lagrange.1 = (f32[16,4,8,128]{3,2,1,0:T(8,128)S(1)}, f32[3,4,8,128]{3,2,1,0:T(8,128)S(1)}, f32[9,8,128]{2,1,0:T(8,128)S(1)}, f32[9,8,128]{2,1,0:T(8,128)S(1)}, ...) custom-call(f32[16,4,8,128]{3,2,1,0:T(8,128)S(1)} %bitcast.5, f32[81,4,8,128]{3,2,1,0:T(8,128)S(1)} %bitcast.4), custom_call_target="tpu_custom_call" | custom-call | tf_op jit(solution)/shard_map/lagrange/pallas_call | solution.py:182
  3.8 3.0 %collective-permute-start = (f32[9,8,128]{2,1,0:T(8,128)S(1)}, f32[9,8,128]{2,1,0:T(8,128)S(1)}, u32[]{:S(2)}, u32[]{:S(2)}) collective-permute-start(f32[9,8,128]{2,1,0:T(8,128)S(1)} %get-tuple-element.19), channel_id=1, source_target_pairs={{0,4},{4,0},{8,12},{12,8},{16,20},{20,16},{24,28},{28,24},{1,5},{5... | collective-permute-start | bytes 110600 | tf_op jit(solution)/shard_map/ppermute | solution.py:461
  6.8 0.7 %collective-permute-start.1 = (f32[9,8,128]{2,1,0:T(8,128)S(1)}, f32[9,8,128]{2,1,0:T(8,128)S(1)}, u32[]{:S(2)}, u32[]{:S(2)}) collective-permute-start(f32[9,8,128]{2,1,0:T(8,128)S(1)} %get-tuple-element.20), channel_id=1, source_target_pairs={{4,8},{8,4},{12,16},{16,12},{20,24},{24,20},{5,9},{9,5},{13,17},{1... | collective-permute-start | bytes 110600 | tf_op jit(solution)/shard_map/ppermute | solution.py:462
  7.5 0.1 collective-permute-start.2
  7.6 0.7 %collective-permute-start.3 = (f32[9,4,128]{2,1,0:T(4,128)S(1)}, f32[9,4,128]{2,1,0:T(4,128)S(1)}, u32[]{:S(2)}, u32[]{:S(2)}) collective-permute-start(f32[9,4,128]{2,1,0:T(4,128)S(1)} %get-tuple-element.22), channel_id=1, source_target_pairs={{1,2},{2,1},{5,6},{6,5},{9,10},{10,9},{13,14},{14,13},{17,18},{18,... | collective-permute-start | bytes 55304 | tf_op jit(solution)/shard_map/ppermute | solution.py:464
  8.2 0.0 copy-done.4
  8.2 0.1 copy.7.owners_hbm
  8.3 0.4 %collective-permute-done.2.ya_ref = f32[9,4,128]{2,1,0:T(4,128)S(1)} collective-permute-done((f32[9,4,128]{2,1,0:T(4,128)S(1)}, f32[9,4,128]{2,1,0:T(4,128)S(1)}, u32[]{:S(2)}, u32[]{:S(2)}) %collective-permute-start.2) | collective-permute-done | bytes 18464 | tf_op jit(solution)/shard_map/ppermute | solution.py:463
  8.7 0.0 collective-permute-done.3.yb_ref
  8.7 0.0 collective-permute-done.xa_ref
  8.8 0.0 collective-permute-done.1.xb_ref
  8.8 0.0 copy-done.2
  8.8 0.0 copy-done.3
  8.8 1.0 %remap.1 = (f32[16,4,8,128]{3,2,1,0:T(8,128)S(1)}, f32[32,1,128]{2,1,0:T(1,128)S(1)}, f32[1,128]{1,0:T(1,128)S(1)}, f32[4,16,128]{2,1,0:T(8,128)S(1)}, f32[4,16,...) custom-call(f32[16,4,8,128]{3,2,1,0:T(8,128)S(1)} %get-tuple-element.17.state_ref, ...), custom_call_target="tpu_custom_call" | custom-call | tf_op jit(solution)/shard_map/remap/pallas_call | solution.py:375
  9.8 4.4 %collective-permute-start.4 = (f32[4,16,128]{2,1,0:T(8,128)S(1)}, f32[4,16,128]{2,1,0:T(8,128)S(1)}, u32[]{:S(2)}, u32[]{:S(2)}) collective-permute-start(f32[4,16,128]{2,1,0:T(8,128)S(1)} %get-tuple-element.29), channel_id=1, source_target_pairs={{0,1},{1,0},{2,3},{3,2},{4,5},{5,4},{6,7},{7,6},{8,9},{9,8},{10,11... | collective-permute-start | bytes 98312 | tf_op jit(solution)/shard_map/ppermute | solution.py:470
  14.2 1.1 %collective-permute-start.5 = (f32[4,16,128]{2,1,0:T(8,128)S(1)}, f32[4,16,128]{2,1,0:T(8,128)S(1)}, u32[]{:S(2)}, u32[]{:S(2)}) collective-permute-start(f32[4,16,128]{2,1,0:T(8,128)S(1)} %get-tuple-element.30), channel_id=1, source_target_pairs={{0,2},{1,3},{2,0},{3,1},{4,6},{5,7},{6,4},{7,5},{8,10},{9,11},{10,... | collective-permute-start | bytes 98312 | tf_op jit(solution)/shard_map/ppermute | solution.py:470
  15.3 0.3 collective-permute-start.6
  15.7 14.5 %all_to_all.5.total_ref = f32[32,1,128]{2,1,0:T(1,128)S(1)} all-to-all(f32[32,1,128]{2,1,0:T(1,128)S(1)} %get-tuple-element.24), channel_id=1, replica_groups=mesh['px'=8,'py'=4] {'px','py'}, dimensions={0} | all-to-all | bytes 32768 | tf_op jit(solution)/shard_map/all_to_all | solution.py:472
  30.2 0.9 %scale.1 = (f32[16,4,8,128]{3,2,1,0:T(8,128)}, f32[2,128]{1,0:T(2,128)S(1)}) custom-call(f32[16,4,8,128]{3,2,1,0:T(8,128)S(1)} %get-tuple-element.23.state_ref, f32[32,1,128]{2,1,0:T(1,128)S(1)} %all_to_all.5.total_ref, f32[1,128]{1,0:T(1,128)S(1)} %get-tuple-element.25.goal_ref), custom_call_target="tpu_custom_call" | custom-call | tf_op jit(solution)/shard_map/scale/pallas_call | solution.py:414
  31.1 0.0 collective-permute-done.4.refs_1_
  31.1 0.0 collective-permute-done.5.refs_2_
  31.1 0.0 collective-permute-done.6.refs_3_
  31.1 0.7 %settle.1 = f32[16,16,128]{2,1,0:T(8,128)} custom-call(f32[2,128]{1,0:T(2,128)S(1)} %get-tuple-element.27.scale_ref, f32[4,16,128]{2,1,0:T(8,128)S(1)} %get-tuple-element.28.refs_0_, f32[4,16,128]{2,1,0:T(8,128)S(1)} %collective-permute-done.4.refs_1_, f32[4,16,128]{2,1,0:T(8,128)S(1)} %collective-permute-done.5.refs_2_, ...), custom_call_target="tpu_custom_call" | custom-call | tf_op jit(solution)/shard_map/settle/pallas_call | solution.py:438
Async XLA Ops:
  0.6 7.6 %copy-start.4 = (s32[1,8,1]{1,2,0:T(1,128)S(1)}, s32[1,8,1]{1,2,0:T(1,128)}, u32[]{:S(2)}) copy-start(s32[1,8,1]{1,2,0:T(1,128)} %param.9) | copy-start | bytes 100
  0.6 8.1 %copy-start.2 = (s32[1,8]{1,0:T(1,128)S(1)}, s32[1,8]{1,0:T(1,128)}, u32[]{:S(2)}) copy-start(s32[1,8]{1,0:T(1,128)} %blocks_hbm.1) | copy-start | bytes 100
  0.7 8.1 %copy-start.3 = (f32[2]{0:T(128)S(1)}, f32[2]{0:T(128)}, u32[]{:S(2)}) copy-start(f32[2]{0:T(128)} %targets_hbm.1) | copy-start | bytes 28
  0.7 1.3 %copy-start = (f32[3,3,3,3,4,8,128]{6,5,4,3,2,1,0:T(8,128)S(1)}, f32[3,3,3,3,4,8,128]{6,5,4,3,2,1,0:T(8,128)}, u32[]{:S(2)}) copy-start(f32[3,3,3,3,4,8,128]{6,5,4,3,2,1,0:T(8,128)} %param.6) | copy-start | bytes 3981316
  2.0 0.9 %copy-start.1 = (f32[2,2,2,2,4,8,128]{6,5,4,3,2,1,0:T(8,128)S(1)}, f32[2,2,2,2,4,8,128]{6,5,4,3,2,1,0:T(8,128)}, u32[]{:S(2)}) copy-start(f32[2,2,2,2,4,8,128]{6,5,4,3,2,1,0:T(8,128)} %param.5) | copy-start | bytes 786436
  3.8 5.0 %collective-permute-start = (f32[9,8,128]{2,1,0:T(8,128)S(1)}, f32[9,8,128]{2,1,0:T(8,128)S(1)}, u32[]{:S(2)}, u32[]{:S(2)}) collective-permute-start(f32[9,8,128]{2,1,0:T(8,128)S(1)} %get-tuple-element.19), channel_id=1, source_target_pairs={{0,4},{4,0},{8,12},{12,8},{16,20},{20,16},{24,28},{28,24},{1,5},{5... | collective-permute-start | bytes 110600 | tf_op jit(solution)/shard_map/ppermute | solution.py:461
  6.8 1.9 %collective-permute-start.1 = (f32[9,8,128]{2,1,0:T(8,128)S(1)}, f32[9,8,128]{2,1,0:T(8,128)S(1)}, u32[]{:S(2)}, u32[]{:S(2)}) collective-permute-start(f32[9,8,128]{2,1,0:T(8,128)S(1)} %get-tuple-element.20), channel_id=1, source_target_pairs={{4,8},{8,4},{12,16},{16,12},{20,24},{24,20},{5,9},{9,5},{13,17},{1... | collective-permute-start | bytes 110600 | tf_op jit(solution)/shard_map/ppermute | solution.py:462
  7.5 1.3 %collective-permute-start.2 = (f32[9,4,128]{2,1,0:T(4,128)S(1)}, f32[9,4,128]{2,1,0:T(4,128)S(1)}, u32[]{:S(2)}, u32[]{:S(2)}) collective-permute-start(f32[9,4,128]{2,1,0:T(4,128)S(1)} %get-tuple-element.21), channel_id=1, source_target_pairs={{0,1},{1,0},{2,3},{3,2},{4,5},{5,4},{6,7},{7,6},{8,9},{9,8},{10,11... | collective-permute-start | bytes 55304 | tf_op jit(solution)/shard_map/ppermute | solution.py:463
  7.6 1.2 %collective-permute-start.3 = (f32[9,4,128]{2,1,0:T(4,128)S(1)}, f32[9,4,128]{2,1,0:T(4,128)S(1)}, u32[]{:S(2)}, u32[]{:S(2)}) collective-permute-start(f32[9,4,128]{2,1,0:T(4,128)S(1)} %get-tuple-element.22), channel_id=1, source_target_pairs={{1,2},{2,1},{5,6},{6,5},{9,10},{10,9},{13,14},{14,13},{17,18},{18,... | collective-permute-start | bytes 55304 | tf_op jit(solution)/shard_map/ppermute | solution.py:464
  9.8 21.3 %collective-permute-start.4 = (f32[4,16,128]{2,1,0:T(8,128)S(1)}, f32[4,16,128]{2,1,0:T(8,128)S(1)}, u32[]{:S(2)}, u32[]{:S(2)}) collective-permute-start(f32[4,16,128]{2,1,0:T(8,128)S(1)} %get-tuple-element.29), channel_id=1, source_target_pairs={{0,1},{1,0},{2,3},{3,2},{4,5},{5,4},{6,7},{7,6},{8,9},{9,8},{10,11... | collective-permute-start | bytes 98312 | tf_op jit(solution)/shard_map/ppermute | solution.py:470
  14.2 16.9 %collective-permute-start.5 = (f32[4,16,128]{2,1,0:T(8,128)S(1)}, f32[4,16,128]{2,1,0:T(8,128)S(1)}, u32[]{:S(2)}, u32[]{:S(2)}) collective-permute-start(f32[4,16,128]{2,1,0:T(8,128)S(1)} %get-tuple-element.30), channel_id=1, source_target_pairs={{0,2},{1,3},{2,0},{3,1},{4,6},{5,7},{6,4},{7,5},{8,10},{9,11},{10,... | collective-permute-start | bytes 98312 | tf_op jit(solution)/shard_map/ppermute | solution.py:470
  15.3 15.8 %collective-permute-start.6 = (f32[4,16,128]{2,1,0:T(8,128)S(1)}, f32[4,16,128]{2,1,0:T(8,128)S(1)}, u32[]{:S(2)}, u32[]{:S(2)}) collective-permute-start(f32[4,16,128]{2,1,0:T(8,128)S(1)} %get-tuple-element.31), channel_id=1, source_target_pairs={{0,3},{1,2},{2,1},{3,0},{4,7},{5,6},{6,5},{7,4},{8,11},{9,10},{10,... | collective-permute-start | bytes 98312 | tf_op jit(solution)/shard_map/ppermute | solution.py:470

commit v2 on v1

--- a/solution.py
+++ b/solution.py
@@ -18,7 +18,7 @@
 
 
 def in_place():
-    return pl.BlockSpec(memory_space=pl.ANY)
+    return pl.BlockSpec(memory_space=pltpu.HBM)
 
 
 def shape_of(*shape):
@@ -29,17 +29,19 @@
     return pltpu.CompilerParams(vmem_limit_bytes=16 * 1024 * 1024)
 
 
-def paired(size, first):
+def exchanges(counts, axis, first):
     pairs = []
-    for low in range(first, size - 1, 2):
-        pairs += [(low, low + 1), (low + 1, low)]
+    for i in range(counts[0]):
+        for j in range(counts[1]):
+            place = [i, j]
+            partner = list(place)
+            along_axis = place[axis] + 1 if (place[axis] - first) % 2 == 0 else place[axis] - 1
+            if 0 <= along_axis < counts[axis]:
+                partner[axis] = along_axis
+            elif place[1 - axis] ^ 1 < counts[1 - axis]:
+                partner[1 - axis] = place[1 - axis] ^ 1
+            pairs.append((i * counts[1] + j, partner[0] * counts[1] + partner[1]))
     return pairs
-
-
-def partner_of(index, hop, size):
-    if size & (size - 1) == 0:
-        return index ^ hop
-    return lax.rem(index + hop, size)
 
 
 def giver_of(index, hop, size):
@@ -198,7 +200,10 @@
         ],
         compiler_params=kernel_options(),
         name="lagrange",
-    )(conserved.reshape((16,) + sizes), velocity.reshape((81,) + sizes))
+    )(
+        pltpu.with_memory_space_constraint(conserved.reshape((16,) + sizes), pltpu.HBM),
+        pltpu.with_memory_space_constraint(velocity.reshape((81,) + sizes), pltpu.HBM),
+    )
 
 
 def remap_kernel(
@@ -230,14 +235,26 @@
         copy.start()
     lane = lax.broadcasted_iota(jnp.int32, (width_y, depth_z), 1)
     row = lax.broadcasted_iota(jnp.int32, (width_y, depth_z), 0)
-    even_x = lax.rem(lax.axis_index("px"), 2) == 0
-    even_y = lax.rem(lax.axis_index("py"), 2) == 0
+    index_x = lax.axis_index("px")
+    index_y = lax.axis_index("py")
+    even_x = lax.rem(index_x, 2) == 0
+    even_y = lax.rem(index_y, 2) == 0
+    some_below_x, some_above_x = index_x > 0, index_x < lax.axis_size("px") - 1
+    some_below_y, some_above_y = index_y > 0, index_y < count_py - 1
 
     def below_x(k):
-        return jnp.where(even_x, xb_ref[k], xa_ref[k])
+        return jnp.where(some_below_x, jnp.where(even_x, xb_ref[k], xa_ref[k]), 0.0)
 
     def above_x(k):
-        return jnp.where(even_x, xa_ref[k], xb_ref[k])
+        return jnp.where(some_above_x, jnp.where(even_x, xa_ref[k], xb_ref[k]), 0.0)
+
+    def below_y(k, x):
+        ya, yb = ya_ref[k, pl.ds(x, 1), :], yb_ref[k, pl.ds(x, 1), :]
+        return jnp.where(some_below_y, jnp.where(even_y, yb, ya), 0.0)
+
+    def above_y(k, x):
+        ya, yb = ya_ref[k, pl.ds(x, 1), :], yb_ref[k, pl.ds(x, 1), :]
+        return jnp.where(some_above_y, jnp.where(even_y, ya, yb), 0.0)
 
     def split(speed):
         return jnp.maximum(speed, 0.0), jnp.minimum(speed, 0.0)
@@ -255,8 +272,7 @@
         speed_x, speed_y, speed_z = (relative_ref[d, x] for d in range(3))
         beyond = above_x(8) if x == width_x - 1 else relative_ref[0, x + 1]
         upper_x_rate = split(0.5 * (speed_x + beyond))
-        y_below = jnp.where(even_y, yb_ref[8, pl.ds(x, 1), :], ya_ref[8, pl.ds(x, 1), :])
-        y_above = jnp.where(even_y, ya_ref[8, pl.ds(x, 1), :], yb_ref[8, pl.ds(x, 1), :])
+        y_below, y_above = below_y(8, x), above_y(8, x)
         lower_y_rate = split(
             0.5 * (jnp.where(row == 0, y_below, pltpu.roll(speed_y, 1, 0)) + speed_y)
         )
@@ -302,14 +318,10 @@
                     low = a * 4 + c
                     high = low + 2
                     k = field * 4 + a * 2 + c
-                    ya = ya_ref[k, pl.ds(x, 1), :]
-                    yb = yb_ref[k, pl.ds(x, 1), :]
-                    left = jnp.where(
-                        row == 0, jnp.where(even_y, yb, ya), pltpu.roll(state[high], 1, 0)
-                    )
+                    left = jnp.where(row == 0, below_y(k, x), pltpu.roll(state[high], 1, 0))
                     right = jnp.where(
                         row == width_y - 1,
-                        jnp.where(even_y, ya, yb),
+                        above_y(k, x),
                         pltpu.roll(state[low], width_y - 1, 0),
                     )
                     update(
@@ -341,7 +353,7 @@
         copy.wait()
     half = lax.broadcasted_iota(jnp.int32, goal_ref.shape, 1) < depth_z // 2
     goal_ref[...] = jnp.where(half, targets_ref[0], targets_ref[1])
-    place = lax.axis_index("py")
+    place = index_y
     rows = out_ref.reshape(16 * width_x * width_y, depth_z)
     owners = [owners_ref[0, entry, 0] for entry in range(entries)]
     for entry in range(entries):
@@ -457,11 +469,10 @@
     device_count = count_px * count_py
     total_nodes = 8.0 * math.prod(conserved.shape[4:]) * device_count
     state, relative, xa, xb, ya, yb = lagrange_call(conserved, velocity)
-    halos = (
-        lax.ppermute(xa, "px", paired(count_px, 0)),
-        lax.ppermute(xb, "px", paired(count_px, 1)),
-        lax.ppermute(ya, "py", paired(count_py, 0)),
-        lax.ppermute(yb, "py", paired(count_py, 1)),
+    counts = (count_px, count_py)
+    halos = tuple(
+        lax.ppermute(message, ("px", "py"), exchanges(counts, axis, first))
+        for message, axis, first in ((xa, 0, 0), (xb, 0, 1), (ya, 1, 0), (yb, 1, 1))
     )
     remapped, total, goal, *chunks = remap_call(
         state, relative, halos, handoff_blocks, handoff_owner, targets, device_count, count_py

time: 32 us -> 26.8 us (0.84)
  blocking collectives: 14.5 us -> 12 us
  starting transfers between devices: 10.3 us -> 7.99 us
  local copies, waits for them, and re-layouts: 2.38 us -> 0.09 us
  waiting for transfers between devices: 0.45 us -> 1.67 us
  Pallas kernels: 3.42 us -> 4.25 us
    ppermute x3, starting transfers between devices: 5.87 us -> 1.92 us  [body(): lax.ppermute(chunks[hop], 'py', hop_pairs(count_py, hop))]
    all_to_all x1, blocking collectives: 14.5 us -> 12 us  [body(): gathered = lax.all_to_all(total, ('px', 'py'), 0, 0, tiled=True)]
    unnamed x11 -> x7, local copies, waits for them, and re-layouts: 2.38 us -> 0.09 us
    ppermute x4, starting transfers between devices: 4.41 us -> 6.07 us  [body(): lax.ppermute(message, ('px', 'py'), exchanges(counts, axis, first))]
    ppermute x4, waiting for transfers between devices: 0.44 us -> 1.66 us  [body(): lax.ppermute(message, ('px', 'py'), exchanges(counts, axis, first))]
    pallas_call x1, Pallas kernels: 0.84 us -> 1.66 us  [lagrange_call(): pl.pallas_call(functools.partial(lagrange_kernel, sizes), out_shape=(shap...]
where the time goes in v2:
time: 26.8 us; the launch traced here: 26.7 us
  blocking collectives  12 us (45%)
  starting transfers between devices  7.99 us (30%)
  Pallas kernels  4.25 us (16%)
  waiting for transfers between devices  1.67 us (6%)
  between operations  0.7 us (3%)
    all_to_all x1, blocking collectives, body(): gathered = lax.all_to_all(total, ('px', 'py'), 0, 0, tiled=True)  12 us
    ppermute x4, starting transfers between devices, body(): lax.ppermute(message, ('px', 'py'), exchanges(counts, axis, first))  6.07 us
    ppermute x3, starting transfers between devices, body(): lax.ppermute(chunks[hop], 'py', hop_pairs(count_py, hop))  1.92 us
    ppermute x4, waiting for transfers between devices, body(): lax.ppermute(message, ('px', 'py'), exchanges(counts, axis, first))  1.66 us
    pallas_call x1, Pallas kernels, lagrange_call(): pl.pallas_call(functools.partial(lagrange_kernel, sizes), out_shape=(shap...  1.66 us
    pallas_call x1, Pallas kernels, remap_call(): pl.pallas_call(functools.partial(remap_kernel, sizes, count_py, entries,...  1.01 us
    pallas_call x1, Pallas kernels, scale_call(): pl.pallas_call(functools.partial(scale_kernel, total_nodes), out_shape=(s...  0.91 us
    pallas_call x1, Pallas kernels, settle_call(): pl.pallas_call(functools.partial(settle_kernel, count_py, capacity), out_...  0.67 us
  transfers between devices with their start and end apart: 7, of which 1 were waited for; matrix products, arithmetic and copies ran while one was open for 0% of the time, Pallas kernels for 3%

profile of v2, /device:TPU:0, one launch (start us, length us, event | category | flops | bytes accessed | tf_op | source)
XLA Modules:
  0.0 26.7 jit_solution(6138539651839378655)
XLA Ops:
  0.6 0.0 copy-start.2
  0.6 0.0 copy-start
  0.7 0.0 copy-start.1
  0.7 1.7 %lagrange.1 = (f32[16,4,8,128]{3,2,1,0:T(8,128)S(1)}, f32[3,4,8,128]{3,2,1,0:T(8,128)S(1)}, f32[9,8,128]{2,1,0:T(8,128)S(1)}, f32[9,8,128]{2,1,0:T(8,128)S(1)}, ...) custom-call(f32[16,4,8,128]{3,2,1,0:T(8,128)} %bitcast.5, f32[81,4,8,128]{3,2,1,0:T(8,128)} %bitcast.4), custom_call_target="tpu_custom_call" | custom-call | tf_op jit(solution)/shard_map/lagrange/pallas_call | solution.py:184
  2.3 3.0 %collective-permute-start = (f32[9,8,128]{2,1,0:T(8,128)S(1)}, f32[9,8,128]{2,1,0:T(8,128)S(1)}, u32[]{:S(2)}, u32[]{:S(2)}) collective-permute-start(f32[9,8,128]{2,1,0:T(8,128)S(1)} %get-tuple-element.19), channel_id=1, source_target_pairs={{0,4},{1,5},{2,6},{3,7},{4,0},{5,1},{6,2},{7,3},{8,12},{9,13},{10,... | collective-permute-start | bytes 110600 | tf_op jit(solution)/shard_map/ppermute | solution.py:474
  5.4 0.0 collective-permute-start.1
  5.4 0.5 %collective-permute-start.2 = (f32[9,4,128]{2,1,0:T(4,128)S(1)}, f32[9,4,128]{2,1,0:T(4,128)S(1)}, u32[]{:S(2)}, u32[]{:S(2)}) collective-permute-start(f32[9,4,128]{2,1,0:T(4,128)S(1)} %get-tuple-element.21), channel_id=1, source_target_pairs={{0,1},{1,0},{2,3},{3,2},{4,5},{5,4},{6,7},{7,6},{8,9},{9,8},{10,11... | collective-permute-start | bytes 55304 | tf_op jit(solution)/shard_map/ppermute | solution.py:474
  5.9 2.5 %collective-permute-start.3 = (f32[9,4,128]{2,1,0:T(4,128)S(1)}, f32[9,4,128]{2,1,0:T(4,128)S(1)}, u32[]{:S(2)}, u32[]{:S(2)}) collective-permute-start(f32[9,4,128]{2,1,0:T(4,128)S(1)} %get-tuple-element.22), channel_id=1, source_target_pairs={{0,4},{1,2},{2,1},{3,7},{4,0},{5,6},{6,5},{7,3},{8,12},{9,10},{10,... | collective-permute-start | bytes 55304 | tf_op jit(solution)/shard_map/ppermute | solution.py:474
  8.4 0.0 copy-done.2
  8.4 0.1 copy.7.owners_hbm
  8.5 0.0 collective-permute-done.2.ya_ref
  8.5 1.7 %collective-permute-done.3.yb_ref = f32[9,4,128]{2,1,0:T(4,128)S(1)} collective-permute-done((f32[9,4,128]{2,1,0:T(4,128)S(1)}, f32[9,4,128]{2,1,0:T(4,128)S(1)}, u32[]{:S(2)}, u32[]{:S(2)}) %collective-permute-start.3) | collective-permute-done | bytes 18464 | tf_op jit(solution)/shard_map/ppermute | solution.py:474
  10.1 0.0 collective-permute-done.xa_ref
  10.1 0.0 collective-permute-done.1.xb_ref
  10.1 0.0 copy-done
  10.1 0.0 copy-done.1
  10.2 1.0 %remap.1 = (f32[16,4,8,128]{3,2,1,0:T(8,128)S(1)}, f32[32,1,128]{2,1,0:T(1,128)S(1)}, f32[1,128]{1,0:T(1,128)S(1)}, f32[4,16,128]{2,1,0:T(8,128)S(1)}, f32[4,16,...) custom-call(f32[16,4,8,128]{3,2,1,0:T(8,128)S(1)} %get-tuple-element.17.state_ref, ...), custom_call_target="tpu_custom_call" | custom-call | tf_op jit(solution)/shard_map/remap/pallas_call | solution.py:387
  11.2 0.1 collective-permute-start.4
  11.3 1.1 %collective-permute-start.5 = (f32[4,16,128]{2,1,0:T(8,128)S(1)}, f32[4,16,128]{2,1,0:T(8,128)S(1)}, u32[]{:S(2)}, u32[]{:S(2)}) collective-permute-start(f32[4,16,128]{2,1,0:T(8,128)S(1)} %get-tuple-element.30), channel_id=1, source_target_pairs={{0,2},{1,3},{2,0},{3,1},{4,6},{5,7},{6,4},{7,5},{8,10},{9,11},{10,... | collective-permute-start | bytes 98312 | tf_op jit(solution)/shard_map/ppermute | solution.py:481
  12.4 0.7 %collective-permute-start.6 = (f32[4,16,128]{2,1,0:T(8,128)S(1)}, f32[4,16,128]{2,1,0:T(8,128)S(1)}, u32[]{:S(2)}, u32[]{:S(2)}) collective-permute-start(f32[4,16,128]{2,1,0:T(8,128)S(1)} %get-tuple-element.31), channel_id=1, source_target_pairs={{0,3},{1,2},{2,1},{3,0},{4,7},{5,6},{6,5},{7,4},{8,11},{9,10},{10,... | collective-permute-start | bytes 98312 | tf_op jit(solution)/shard_map/ppermute | solution.py:481
  13.1 12.0 %all_to_all.5.total_ref = f32[32,1,128]{2,1,0:T(1,128)S(1)} all-to-all(f32[32,1,128]{2,1,0:T(1,128)S(1)} %get-tuple-element.24), channel_id=1, replica_groups=mesh['px'=8,'py'=4] {'px','py'}, dimensions={0} | all-to-all | bytes 32768 | tf_op jit(solution)/shard_map/all_to_all | solution.py:483
  25.1 0.9 %scale.1 = (f32[16,4,8,128]{3,2,1,0:T(8,128)}, f32[2,128]{1,0:T(2,128)S(1)}) custom-call(f32[16,4,8,128]{3,2,1,0:T(8,128)S(1)} %get-tuple-element.23.state_ref, f32[32,1,128]{2,1,0:T(1,128)S(1)} %all_to_all.5.total_ref, f32[1,128]{1,0:T(1,128)S(1)} %get-tuple-element.25.goal_ref), custom_call_target="tpu_custom_call" | custom-call | tf_op jit(solution)/shard_map/scale/pallas_call | solution.py:426
  26.0 0.0 collective-permute-done.4.refs_1_
  26.0 0.0 collective-permute-done.5.refs_2_
  26.0 0.0 collective-permute-done.6.refs_3_
  26.0 0.7 %settle.1 = f32[16,16,128]{2,1,0:T(8,128)} custom-call(f32[2,128]{1,0:T(2,128)S(1)} %get-tuple-element.27.scale_ref, f32[4,16,128]{2,1,0:T(8,128)S(1)} %get-tuple-element.28.refs_0_, f32[4,16,128]{2,1,0:T(8,128)S(1)} %collective-permute-done.4.refs_1_, f32[4,16,128]{2,1,0:T(8,128)S(1)} %collective-permute-done.5.refs_2_, ...), custom_call_target="tpu_custom_call" | custom-call | tf_op jit(solution)/shard_map/settle/pallas_call | solution.py:450
Async XLA Ops:
  0.6 7.8 %copy-start.2 = (s32[1,8,1]{1,2,0:T(1,128)S(1)}, s32[1,8,1]{1,2,0:T(1,128)}, u32[]{:S(2)}) copy-start(s32[1,8,1]{1,2,0:T(1,128)} %param.9) | copy-start | bytes 100
  0.6 9.5 %copy-start = (s32[1,8]{1,0:T(1,128)S(1)}, s32[1,8]{1,0:T(1,128)}, u32[]{:S(2)}) copy-start(s32[1,8]{1,0:T(1,128)} %blocks_hbm.1) | copy-start | bytes 100
  0.7 9.5 %copy-start.1 = (f32[2]{0:T(128)S(1)}, f32[2]{0:T(128)}, u32[]{:S(2)}) copy-start(f32[2]{0:T(128)} %targets_hbm.1) | copy-start | bytes 28
  2.3 7.8 %collective-permute-start = (f32[9,8,128]{2,1,0:T(8,128)S(1)}, f32[9,8,128]{2,1,0:T(8,128)S(1)}, u32[]{:S(2)}, u32[]{:S(2)}) collective-permute-start(f32[9,8,128]{2,1,0:T(8,128)S(1)} %get-tuple-element.19), channel_id=1, source_target_pairs={{0,4},{1,5},{2,6},{3,7},{4,0},{5,1},{6,2},{7,3},{8,12},{9,13},{10,... | collective-permute-start | bytes 110600 | tf_op jit(solution)/shard_map/ppermute | solution.py:474
  5.4 4.8 %collective-permute-start.1 = (f32[9,8,128]{2,1,0:T(8,128)S(1)}, f32[9,8,128]{2,1,0:T(8,128)S(1)}, u32[]{:S(2)}, u32[]{:S(2)}) collective-permute-start(f32[9,8,128]{2,1,0:T(8,128)S(1)} %get-tuple-element.20), channel_id=1, source_target_pairs={{0,1},{1,0},{2,3},{3,2},{4,8},{5,9},{6,10},{7,11},{8,4},{9,5},{10,... | collective-permute-start | bytes 110600 | tf_op jit(solution)/shard_map/ppermute | solution.py:474
  5.4 3.1 %collective-permute-start.2 = (f32[9,4,128]{2,1,0:T(4,128)S(1)}, f32[9,4,128]{2,1,0:T(4,128)S(1)}, u32[]{:S(2)}, u32[]{:S(2)}) collective-permute-start(f32[9,4,128]{2,1,0:T(4,128)S(1)} %get-tuple-element.21), channel_id=1, source_target_pairs={{0,1},{1,0},{2,3},{3,2},{4,5},{5,4},{6,7},{7,6},{8,9},{9,8},{10,11... | collective-permute-start | bytes 55304 | tf_op jit(solution)/shard_map/ppermute | solution.py:474
  5.9 4.3 %collective-permute-start.3 = (f32[9,4,128]{2,1,0:T(4,128)S(1)}, f32[9,4,128]{2,1,0:T(4,128)S(1)}, u32[]{:S(2)}, u32[]{:S(2)}) collective-permute-start(f32[9,4,128]{2,1,0:T(4,128)S(1)} %get-tuple-element.22), channel_id=1, source_target_pairs={{0,4},{1,2},{2,1},{3,7},{4,0},{5,6},{6,5},{7,3},{8,12},{9,10},{10,... | collective-permute-start | bytes 55304 | tf_op jit(solution)/shard_map/ppermute | solution.py:474
  11.2 14.8 %collective-permute-start.4 = (f32[4,16,128]{2,1,0:T(8,128)S(1)}, f32[4,16,128]{2,1,0:T(8,128)S(1)}, u32[]{:S(2)}, u32[]{:S(2)}) collective-permute-start(f32[4,16,128]{2,1,0:T(8,128)S(1)} %get-tuple-element.29), channel_id=1, source_target_pairs={{0,1},{1,0},{2,3},{3,2},{4,5},{5,4},{6,7},{7,6},{8,9},{9,8},{10,11... | collective-permute-start | bytes 98312 | tf_op jit(solution)/shard_map/ppermute | solution.py:481
  11.3 14.7 %collective-permute-start.5 = (f32[4,16,128]{2,1,0:T(8,128)S(1)}, f32[4,16,128]{2,1,0:T(8,128)S(1)}, u32[]{:S(2)}, u32[]{:S(2)}) collective-permute-start(f32[4,16,128]{2,1,0:T(8,128)S(1)} %get-tuple-element.30), channel_id=1, source_target_pairs={{0,2},{1,3},{2,0},{3,1},{4,6},{5,7},{6,4},{7,5},{8,10},{9,11},{10,... | collective-permute-start | bytes 98312 | tf_op jit(solution)/shard_map/ppermute | solution.py:481
  12.4 13.6 %collective-permute-start.6 = (f32[4,16,128]{2,1,0:T(8,128)S(1)}, f32[4,16,128]{2,1,0:T(8,128)S(1)}, u32[]{:S(2)}, u32[]{:S(2)}) collective-permute-start(f32[4,16,128]{2,1,0:T(8,128)S(1)} %get-tuple-element.31), channel_id=1, source_target_pairs={{0,3},{1,2},{2,1},{3,0},{4,7},{5,6},{6,5},{7,4},{8,11},{9,10},{10,... | collective-permute-start | bytes 98312 | tf_op jit(solution)/shard_map/ppermute | solution.py:481

commit v3 on v2

--- a/solution.py
+++ b/solution.py
@@ -7,6 +7,7 @@
 from jax.experimental import pallas as pl
 from jax.experimental.pallas import tpu as pltpu
 from jax.sharding import PartitionSpec as P
+
 
 gamma_less = 0.4
 force_step = 0.02
@@ -65,6 +66,14 @@
     return out
 
 
+def added(values):
+    while len(values) > 1:
+        values = [values[i] + values[i + 1] for i in range(0, len(values) - 1, 2)] + (
+            [values[-1]] if len(values) % 2 else []
+        )
+    return values[0]
+
+
 def quadratic_values(first, second, third):
     middle = (1.0 / 6.0) * (first + third) + (2.0 / 3.0) * second
     tilt = gauss_offset * (third - first)
@@ -87,9 +96,12 @@
     xb_ref,
     ya_ref,
     yb_ref,
+    total_hbm,
     motion_ref,
+    total_ref,
     state_sem,
     motion_sem,
+    total_sem,
 ):
     width_x, width_y, depth_z = sizes
     copies = []
@@ -108,10 +120,16 @@
         state_copy.start()
         motion_copy.start()
     lane = lax.broadcasted_iota(jnp.int32, (width_y, depth_z), 1)
+    row = lax.broadcasted_iota(jnp.int32, (width_y, depth_z), 0)
+    index_x, index_y = lax.axis_index("px"), lax.axis_index("py")
+    first_y = jnp.logical_and(row == 0, index_y == 0)
+    last_y = jnp.logical_and(row == width_y - 1, index_y == lax.axis_size("py") - 1)
+    totals = [None, None]
     for x in range(width_x):
         copies[x][0].wait()
         copies[x][1].wait()
         divergence = [None] * 8
+        motion = []
         for component in range(3):
 
             def node(a, b, c):
@@ -145,7 +163,8 @@
             mean = total * (1.0 / 27.0)
             before = jnp.where(lane == 0, 0.0, pltpu.roll(mean, 1, 1))
             after = jnp.where(lane == depth_z - 1, 0.0, pltpu.roll(mean, depth_z - 1, 1))
-            relative_ref[component, x] = mean - 0.25 * ((before + 2.0 * mean) + after)
+            motion.append(mean - 0.25 * ((before + 2.0 * mean) + after))
+            relative_ref[component, x] = motion[component]
         energy = [state_ref[8 + corner, x] for corner in range(8)]
         work = energy
         for direction in range(3):
@@ -153,16 +172,47 @@
         work = [(gamma_less * work[point]) * divergence[point] for point in range(8)]
         for direction in range(3):
             work = along(work, direction, lambda p, q: lifted(p, q, 3.0 * gauss_offset))
+        energy = [energy[corner] - force_step * work[corner] for corner in range(8)]
         for corner in range(8):
-            state_ref[8 + corner, x] = energy[corner] - force_step * work[corner]
-    odd_x = lax.rem(lax.axis_index("px"), 2)
+            state_ref[8 + corner, x] = energy[corner]
+        half_motion = [0.5 * speed for speed in motion]
+        entering = [
+            jnp.where(index_x == 0, jnp.minimum(half_motion[0], 0.0), 0.0) if x == 0 else None,
+            jnp.where(first_y, jnp.minimum(half_motion[1], 0.0), 0.0),
+            jnp.where(lane == 0, jnp.minimum(half_motion[2], 0.0), 0.0),
+        ]
+        leaving = [
+            jnp.where(index_x == lax.axis_size("px") - 1, jnp.maximum(half_motion[0], 0.0), 0.0)
+            if x == width_x - 1
+            else None,
+            jnp.where(last_y, jnp.maximum(half_motion[1], 0.0), 0.0),
+            jnp.where(lane == depth_z - 1, jnp.maximum(half_motion[2], 0.0), 0.0),
+        ]
+        for field in range(2):
+            values = energy if field else [state_ref[corner, x] for corner in range(8)]
+            part = None
+            for direction in range(3):
+                stride = (4, 2, 1)[direction]
+                low = added([values[k] for k in range(8) if not k & stride])
+                high = added([values[k] for k in range(8) if k & stride])
+                if part is None:
+                    part = low + high
+                if entering[direction] is not None:
+                    part = part + entering[direction] * low
+                if leaving[direction] is not None:
+                    part = part - leaving[direction] * high
+            totals[field] = part if totals[field] is None else totals[field] + part
+    total_ref[...] = jnp.broadcast_to(folded(totals)[None], total_ref.shape)
+    total_copy = pltpu.make_async_copy(total_ref, total_hbm, total_sem)
+    total_copy.start()
+    odd_x = lax.rem(index_x, 2)
     for out_ref, side in ((xa_ref, 1 - odd_x), (xb_ref, odd_x)):
         place = side * (width_x - 1)
         for field in range(2):
             for k in range(4):
                 out_ref[field * 4 + k] = state_ref[field * 8 + side * 4 + k, place]
         out_ref[8] = relative_ref[0, place]
-    odd_y = lax.rem(lax.axis_index("py"), 2)
+    odd_y = lax.rem(index_y, 2)
     state_rows = state_ref.reshape(16 * width_x * width_y, depth_z)
     relative_rows = relative_ref.reshape(3 * width_x * width_y, depth_z)
     column = width_x * width_y
@@ -176,9 +226,10 @@
                         pl.ds(start, width_x, stride=width_y), :
                     ]
         out_ref[8] = relative_rows[pl.ds(column + place, width_x, stride=width_y), :]
-
-
-def lagrange_call(conserved, velocity):
+    total_copy.wait()
+
+
+def lagrange_call(conserved, velocity, device_count):
     width_x, width_y, depth_z = conserved.shape[4:]
     sizes = (width_x, width_y, depth_z)
     return pl.pallas_call(
@@ -190,13 +241,16 @@
             shape_of(9, width_y, depth_z),
             shape_of(9, width_x, depth_z),
             shape_of(9, width_x, depth_z),
+            shape_of(device_count, 1, depth_z),
         ),
         in_specs=[in_place()] * 2,
-        out_specs=(in_vmem(),) * 6,
+        out_specs=(in_vmem(),) * 6 + (in_place(),),
         scratch_shapes=[
             pltpu.VMEM((81,) + sizes, jnp.float32),
+            pltpu.VMEM((device_count, 1, depth_z), jnp.float32),
             pltpu.SemaphoreType.DMA((width_x,)),
             pltpu.SemaphoreType.DMA((width_x,)),
+            pltpu.SemaphoreType.DMA,
         ],
         compiler_params=kernel_options(),
         name="lagrange",
@@ -223,9 +277,9 @@
     *refs,
 ):
     width_x, width_y, depth_z = sizes
-    out_ref, total_ref, goal_ref = refs[:3]
-    send_refs = refs[3 : 3 + count_py]
-    sending, blocks_ref, owners_ref, targets_ref, sems = refs[3 + count_py :]
+    out_ref, goal_ref = refs[:2]
+    send_refs = refs[2 : 2 + count_py]
+    sending, blocks_ref, owners_ref, targets_ref, sems = refs[2 + count_py :]
     copies = [
         pltpu.make_async_copy(blocks_hbm, blocks_ref, sems.at[0]),
         pltpu.make_async_copy(owners_hbm, owners_ref, sems.at[1]),
@@ -260,7 +314,6 @@
         return jnp.maximum(speed, 0.0), jnp.minimum(speed, 0.0)
 
     sending[...] = jnp.zeros(sending.shape, jnp.float32)
-    totals = [None, None]
     speed = relative_ref[0, 0]
     coefficient = split(0.5 * (below_x(8) + speed))
     lower_x = [
@@ -342,20 +395,16 @@
                     upper_z_rate[0] * state[high] + upper_z_rate[1] * right,
                     2,
                 )
-            part = None
             for corner in range(8):
                 out_ref[field * 8 + corner, x] = result[corner]
-                part = result[corner] if part is None else part + result[corner]
-            totals[field] = part if totals[field] is None else totals[field] + part
         lower_x = upper_x
-    total_ref[...] = jnp.broadcast_to(folded(totals)[None], total_ref.shape)
     for copy in copies:
         copy.wait()
     half = lax.broadcasted_iota(jnp.int32, goal_ref.shape, 1) < depth_z // 2
     goal_ref[...] = jnp.where(half, targets_ref[0], targets_ref[1])
     place = index_y
     rows = out_ref.reshape(16 * width_x * width_y, depth_z)
-    owners = [owners_ref[0, entry, 0] for entry in range(entries)]
+    owners = [owners_ref[0, entry] for entry in range(entries)]
     for entry in range(entries):
         slot = jnp.int32(0)
         for earlier in range(entry):
@@ -379,21 +428,17 @@
     return jnp.where(half, rows[0], rows[1])
 
 
-def remap_call(state, relative, halos, blocks, owners, targets, device_count, count_py):
+def remap_call(state, relative, halos, blocks, owners, targets, count_py):
     sizes = state.shape[1:]
-    width_x, width_y, depth_z = sizes
+    _, _, depth_z = sizes
     entries = blocks.shape[1]
     capacity = max(2, 2 * entries // count_py)
     return pl.pallas_call(
         functools.partial(remap_kernel, sizes, count_py, entries, capacity),
-        out_shape=(
-            shape_of(16, *sizes),
-            shape_of(device_count, 1, depth_z),
-            shape_of(1, depth_z),
-        )
+        out_shape=(shape_of(16, *sizes), shape_of(1, depth_z))
         + (shape_of(capacity, 16, depth_z),) * count_py,
         in_specs=[in_vmem()] * 6 + [in_place()] * 3,
-        out_specs=(in_vmem(),) * (3 + count_py),
+        out_specs=(in_vmem(),) * (2 + count_py),
         scratch_shapes=[
             pltpu.VMEM((count_py * capacity, 16, depth_z), jnp.float32),
             pltpu.SMEM(blocks.shape, jnp.int32),
@@ -406,7 +451,9 @@
     )(state, relative, *halos, blocks, owners, targets)
 
 
-def scale_kernel(total_nodes, state_ref, total_ref, goal_ref, fixed_ref, scale_ref):
+def finish_kernel(total_nodes, count_py, capacity, state_ref, total_ref, goal_ref, *refs):
+    chunk_refs = refs[:count_py]
+    fixed_hbm, handed_hbm, fixed_ref, handed_ref, sems = refs[count_py:]
     total = jnp.sum(total_ref[...], axis=0)
     half = lax.broadcasted_iota(jnp.int32, total.shape, 1) < total.shape[1] // 2
     sums = (
@@ -417,44 +464,43 @@
     scale = goal_ref[...] / means
     other = pltpu.roll(scale, scale.shape[1] // 2, 1)
     factors = (jnp.where(half, scale, other), jnp.where(half, other, scale))
+    copies = []
     for field in range(2):
-        scale_ref[pl.ds(field, 1), :] = factors[field]
-        fixed_ref[pl.ds(field * 8, 8)] = state_ref[pl.ds(field * 8, 8)] * factors[field]
-
-
-def scale_call(state, gathered, goal, total_nodes):
-    return pl.pallas_call(
-        functools.partial(scale_kernel, total_nodes),
-        out_shape=(shape_of(*state.shape), shape_of(2, state.shape[-1])),
-        in_specs=[in_vmem()] * 3,
-        out_specs=(in_vmem(),) * 2,
-        compiler_params=kernel_options(),
-        name="scale",
-    )(state, gathered, goal)
-
-
-def settle_kernel(count_py, capacity, scale_ref, *refs):
-    handed_ref = refs[count_py]
+        part = pl.ds(field * 8, 8)
+        fixed_ref[part] = state_ref[part] * factors[field]
+        copies.append(pltpu.make_async_copy(fixed_ref.at[part], fixed_hbm.at[part], sems.at[field]))
+        copies[-1].start()
     place = lax.axis_index("py")
     for hop in range(count_py):
         start = giver_of(place, hop, count_py) * capacity
         for field in range(2):
-            handed_ref[pl.ds(start, capacity), pl.ds(field * 8, 8), :] = (
-                refs[hop][:, pl.ds(field * 8, 8), :] * scale_ref[pl.ds(field, 1), :]
+            part = pl.ds(field * 8, 8)
+            handed_ref[pl.ds(start, capacity), part, :] = (
+                chunk_refs[hop][:, part, :] * factors[field]
             )
-
-
-def settle_call(scale, chunks):
+    copies.append(pltpu.make_async_copy(handed_ref, handed_hbm, sems.at[2]))
+    copies[-1].start()
+    for copy in copies:
+        copy.wait()
+
+
+def finish_call(state, gathered, goal, chunks, total_nodes):
     count_py = len(chunks)
     capacity = chunks[0].shape[0]
+    handed = (count_py * capacity,) + chunks[0].shape[1:]
     return pl.pallas_call(
-        functools.partial(settle_kernel, count_py, capacity),
-        out_shape=shape_of(count_py * capacity, *chunks[0].shape[1:]),
-        in_specs=[in_vmem()] * (1 + count_py),
-        out_specs=in_vmem(),
+        functools.partial(finish_kernel, total_nodes, count_py, capacity),
+        out_shape=(shape_of(*state.shape), shape_of(*handed)),
+        in_specs=[in_vmem()] * (3 + count_py),
+        out_specs=(in_place(),) * 2,
+        scratch_shapes=[
+            pltpu.VMEM(state.shape, jnp.float32),
+            pltpu.VMEM(handed, jnp.float32),
+            pltpu.SemaphoreType.DMA((3,)),
+        ],
         compiler_params=kernel_options(),
-        name="settle",
-    )(scale, *chunks)
+        name="finish",
+    )(state, gathered, goal, *chunks)
 
 
 def hop_pairs(size, hop):
@@ -463,32 +509,36 @@
     return [(i, (i + hop) % size) for i in range(size)]
 
 
-def body(conserved, velocity, targets, handoff_blocks, handoff_owner):
+def step(conserved, velocity, targets, handoff_blocks, handoff_owner):
     count_px = lax.axis_size("px")
     count_py = lax.axis_size("py")
     device_count = count_px * count_py
     total_nodes = 8.0 * math.prod(conserved.shape[4:]) * device_count
-    state, relative, xa, xb, ya, yb = lagrange_call(conserved, velocity)
+    state, relative, xa, xb, ya, yb, total = lagrange_call(conserved, velocity, device_count)
     counts = (count_px, count_py)
-    halos = tuple(
-        lax.ppermute(message, ("px", "py"), exchanges(counts, axis, first))
-        for message, axis, first in ((xa, 0, 0), (xb, 0, 1), (ya, 1, 0), (yb, 1, 1))
+    halos = []
+    for message, axis, first in ((xa, 0, 0), (xb, 0, 1), (ya, 1, 0), (yb, 1, 1)):
+        halos.append(lax.ppermute(message, ("px", "py"), exchanges(counts, axis, first)))
+    gathered = lax.all_to_all(total, ("px", "py"), 0, 0, tiled=True)
+    remapped, goal, *chunks = remap_call(
+        state,
+        relative,
+        halos,
+        handoff_blocks,
+        handoff_owner.reshape(handoff_blocks.shape),
+        targets,
+        count_py,
     )
-    remapped, total, goal, *chunks = remap_call(
-        state, relative, halos, handoff_blocks, handoff_owner, targets, device_count, count_py
-    )
-    received = [chunks[0]] + [
-        lax.ppermute(chunks[hop], "py", hop_pairs(count_py, hop)) for hop in range(1, count_py)
-    ]
-    gathered = lax.all_to_all(total, ("px", "py"), 0, 0, tiled=True)
-    fixed, scale = scale_call(remapped, gathered, goal, total_nodes)
-    handed = settle_call(scale, received)
+    received = [chunks[0]]
+    for hop in range(1, count_py):
+        received.append(lax.ppermute(chunks[hop], "py", hop_pairs(count_py, hop)))
+    fixed, handed = finish_call(remapped, gathered, goal, received, total_nodes)
     return fixed.reshape(conserved.shape), handed[None]
 
 
 def solution(mesh):
     return jax.shard_map(
-        body,
+        step,
         mesh=mesh,
         in_specs=(
             P(None, None, None, None, "px", "py", None),

time: 26.8 us -> 26 us (0.970)
  Pallas kernels: 4.25 us -> 3.47 us
    pallas_call x2 -> x1, Pallas kernels: 1.58 us -> 0.97 us  [finish_call(): pl.pallas_call(functools.partial(finish_kernel, total_nodes, count_py, ca...]
    pallas_call x1, Pallas kernels: 1.01 us -> 0.7 us  [remap_call(): pl.pallas_call(functools.partial(remap_kernel, sizes, count_py, entries,...]
  transfers between devices with their start and end apart: 7 -> 7, of which waited for: 1 -> 1; matrix products, arithmetic and copies ran while one was open for 0% -> 0% of each run, Pallas kernels for 3% -> 0%
where the time goes in v3:
time: 26 us; the launch traced here: 25.9 us
  blocking collectives  11.9 us (46%)
  starting transfers between devices  7.99 us (31%)
  Pallas kernels  3.47 us (13%)
  waiting for transfers between devices  1.75 us (7%)
  between operations  0.71 us (3%)
    all_to_all x1, blocking collectives, step(): gathered = lax.all_to_all(total, ('px', 'py'), 0, 0, tiled=True)  11.9 us
    ppermute x4, starting transfers between devices, step(): lax.ppermute(message, ('px', 'py'), exchanges(counts, axis, first))  6.07 us
    ppermute x3, starting transfers between devices, step(): received.append(lax.ppermute(chunks[hop], 'py', hop_pairs(count_py, hop)))  1.92 us
    pallas_call x1, Pallas kernels, lagrange_call(): pl.pallas_call(functools.partial(lagrange_kernel, sizes), out_shape=(shap...  1.8 us
    ppermute x4, waiting for transfers between devices, step(): lax.ppermute(message, ('px', 'py'), exchanges(counts, axis, first))  1.74 us
    pallas_call x1, Pallas kernels, finish_call(): pl.pallas_call(functools.partial(finish_kernel, total_nodes, count_py, ca...  0.97 us
    pallas_call x1, Pallas kernels, remap_call(): pl.pallas_call(functools.partial(remap_kernel, sizes, count_py, entries,...  0.7 us
  transfers between devices with their start and end apart: 7, of which 1 were waited for; matrix products, arithmetic and copies ran while one was open for 0% of the time, Pallas kernels for 0%

profile of v3, /device:TPU:0, one launch (start us, length us, event | category | flops | bytes accessed | tf_op | source)
XLA Modules:
  0.0 25.9 jit_solution(720129715293810880)
XLA Ops:
  0.6 0.0 copy-start.1
  0.6 0.0 copy-start
  0.7 0.0 copy-start.2
  0.7 1.8 %lagrange.1 = (f32[16,4,8,128]{3,2,1,0:T(8,128)S(1)}, f32[3,4,8,128]{3,2,1,0:T(8,128)S(1)}, f32[9,8,128]{2,1,0:T(8,128)S(1)}, f32[9,8,128]{2,1,0:T(8,128)S(1)}, ...) custom-call(f32[16,4,8,128]{3,2,1,0:T(8,128)} %bitcast.7, f32[81,4,8,128]{3,2,1,0:T(8,128)} %bitcast.6), custom_call_target="tpu_custom_call" | custom-call | tf_op jit(solution)/shard_map/lagrange/pallas_call | solution.py:235
  2.5 3.0 %collective-permute-start = (f32[9,8,128]{2,1,0:T(8,128)S(1)}, f32[9,8,128]{2,1,0:T(8,128)S(1)}, u32[]{:S(2)}, u32[]{:S(2)}) collective-permute-start(f32[9,8,128]{2,1,0:T(8,128)S(1)} %get-tuple-element.19), channel_id=1, source_target_pairs={{0,4},{1,5},{2,6},{3,7},{4,0},{5,1},{6,2},{7,3},{8,12},{9,13},{10,... | collective-permute-start | bytes 110600 | tf_op jit(solution)/shard_map/ppermute | solution.py:521
  5.5 0.0 collective-permute-start.1
  5.5 0.5 %collective-permute-start.2 = (f32[9,4,128]{2,1,0:T(4,128)S(1)}, f32[9,4,128]{2,1,0:T(4,128)S(1)}, u32[]{:S(2)}, u32[]{:S(2)}) collective-permute-start(f32[9,4,128]{2,1,0:T(4,128)S(1)} %get-tuple-element.21), channel_id=1, source_target_pairs={{0,1},{1,0},{2,3},{3,2},{4,5},{5,4},{6,7},{7,6},{8,9},{9,8},{10,11... | collective-permute-start | bytes 55304 | tf_op jit(solution)/shard_map/ppermute | solution.py:521
  6.0 2.5 %collective-permute-start.3 = (f32[9,4,128]{2,1,0:T(4,128)S(1)}, f32[9,4,128]{2,1,0:T(4,128)S(1)}, u32[]{:S(2)}, u32[]{:S(2)}) collective-permute-start(f32[9,4,128]{2,1,0:T(4,128)S(1)} %get-tuple-element.22), channel_id=1, source_target_pairs={{0,4},{1,2},{2,1},{3,7},{4,0},{5,6},{6,5},{7,3},{8,12},{9,10},{10,... | collective-permute-start | bytes 55304 | tf_op jit(solution)/shard_map/ppermute | solution.py:521
  8.5 0.0 collective-permute-done.2.ya_ref
  8.6 1.7 %collective-permute-done.3.yb_ref = f32[9,4,128]{2,1,0:T(4,128)S(1)} collective-permute-done((f32[9,4,128]{2,1,0:T(4,128)S(1)}, f32[9,4,128]{2,1,0:T(4,128)S(1)}, u32[]{:S(2)}, u32[]{:S(2)}) %collective-permute-start.3) | collective-permute-done | bytes 18464 | tf_op jit(solution)/shard_map/ppermute | solution.py:521
  10.3 0.0 collective-permute-done.xa_ref
  10.3 0.0 collective-permute-done.1.xb_ref
  10.3 0.0 copy-done.1
  10.3 0.0 copy-done
  10.3 0.0 copy-done.2
  10.3 0.7 %remap.1 = (f32[16,4,8,128]{3,2,1,0:T(8,128)S(1)}, f32[1,128]{1,0:T(1,128)S(1)}, f32[4,16,128]{2,1,0:T(8,128)S(1)}, f32[4,16,128]{2,1,0:T(8,128)S(1)}, f32[4,16,...) custom-call(f32[16,4,8,128]{3,2,1,0:T(8,128)S(1)} %get-tuple-element.17.state_ref, ...), custom_call_target="tpu_custom_call" | custom-call | tf_op jit(solution)/shard_map/remap/pallas_call | solution.py:436
  11.0 0.1 collective-permute-start.4
  11.1 1.1 %collective-permute-start.5 = (f32[4,16,128]{2,1,0:T(8,128)S(1)}, f32[4,16,128]{2,1,0:T(8,128)S(1)}, u32[]{:S(2)}, u32[]{:S(2)}) collective-permute-start(f32[4,16,128]{2,1,0:T(8,128)S(1)} %get-tuple-element.28), channel_id=1, source_target_pairs={{0,2},{1,3},{2,0},{3,1},{4,6},{5,7},{6,4},{7,5},{8,10},{9,11},{10,... | collective-permute-start | bytes 98312 | tf_op jit(solution)/shard_map/ppermute | solution.py:534
  12.2 0.7 %collective-permute-start.6 = (f32[4,16,128]{2,1,0:T(8,128)S(1)}, f32[4,16,128]{2,1,0:T(8,128)S(1)}, u32[]{:S(2)}, u32[]{:S(2)}) collective-permute-start(f32[4,16,128]{2,1,0:T(8,128)S(1)} %get-tuple-element.29), channel_id=1, source_target_pairs={{0,3},{1,2},{2,1},{3,0},{4,7},{5,6},{6,5},{7,4},{8,11},{9,10},{10,... | collective-permute-start | bytes 98312 | tf_op jit(solution)/shard_map/ppermute | solution.py:534
  12.9 11.9 %all_to_all.5.total_ref = f32[32,1,128]{2,1,0:T(1,128)S(1)} all-to-all(f32[32,1,128]{2,1,0:T(1,128)S(1)} %get-tuple-element.24), channel_id=1, replica_groups=mesh['px'=8,'py'=4] {'px','py'}, dimensions={0} | all-to-all | bytes 32768 | tf_op jit(solution)/shard_map/all_to_all | solution.py:522
  24.9 0.0 collective-permute-done.4.refs_1_
  24.9 0.0 collective-permute-done.5.refs_2_
  24.9 0.0 collective-permute-done.6.refs_3_
  24.9 1.0 %finish.1 = (f32[16,4,8,128]{3,2,1,0:T(8,128)}, f32[16,16,128]{2,1,0:T(8,128)}) custom-call(f32[16,4,8,128]{3,2,1,0:T(8,128)S(1)} %get-tuple-element.23.state_ref, f32[32,1,128]{2,1,0:T(1,128)S(1)} %all_to_all.5.total_ref, f32[1,128]{1,0:T(1,128)S(1)} %get-tuple-element.25.goal_ref, f32[4,16,128]{2,1,0:T(8,128)S(1)} %get-tuple-element.26.refs_0_, ...), custom_call_target="tpu_custom_call" | custom-call | tf_op jit(solution)/shard_map/finish/pallas_call | solution.py:491
Async XLA Ops:
  0.6 9.7 %copy-start.1 = (s32[1,8,1]{1,2,0:T(1,128)S(1)}, s32[1,8,1]{1,2,0:T(1,128)}, u32[]{:S(2)}) copy-start(s32[1,8,1]{1,2,0:T(1,128)} %param.9) | copy-start | bytes 100
  0.6 9.7 %copy-start = (s32[1,8]{1,0:T(1,128)S(1)}, s32[1,8]{1,0:T(1,128)}, u32[]{:S(2)}) copy-start(s32[1,8]{1,0:T(1,128)} %blocks_hbm.1) | copy-start | bytes 100
  0.7 9.7 %copy-start.2 = (f32[2]{0:T(128)S(1)}, f32[2]{0:T(128)}, u32[]{:S(2)}) copy-start(f32[2]{0:T(128)} %targets_hbm.1) | copy-start | bytes 28
  2.5 7.8 %collective-permute-start = (f32[9,8,128]{2,1,0:T(8,128)S(1)}, f32[9,8,128]{2,1,0:T(8,128)S(1)}, u32[]{:S(2)}, u32[]{:S(2)}) collective-permute-start(f32[9,8,128]{2,1,0:T(8,128)S(1)} %get-tuple-element.19), channel_id=1, source_target_pairs={{0,4},{1,5},{2,6},{3,7},{4,0},{5,1},{6,2},{7,3},{8,12},{9,13},{10,... | collective-permute-start | bytes 110600 | tf_op jit(solution)/shard_map/ppermute | solution.py:521
  5.5 4.8 %collective-permute-start.1 = (f32[9,8,128]{2,1,0:T(8,128)S(1)}, f32[9,8,128]{2,1,0:T(8,128)S(1)}, u32[]{:S(2)}, u32[]{:S(2)}) collective-permute-start(f32[9,8,128]{2,1,0:T(8,128)S(1)} %get-tuple-element.20), channel_id=1, source_target_pairs={{0,1},{1,0},{2,3},{3,2},{4,8},{5,9},{6,10},{7,11},{8,4},{9,5},{10,... | collective-permute-start | bytes 110600 | tf_op jit(solution)/shard_map/ppermute | solution.py:521
  5.5 3.0 %collective-permute-start.2 = (f32[9,4,128]{2,1,0:T(4,128)S(1)}, f32[9,4,128]{2,1,0:T(4,128)S(1)}, u32[]{:S(2)}, u32[]{:S(2)}) collective-permute-start(f32[9,4,128]{2,1,0:T(4,128)S(1)} %get-tuple-element.21), channel_id=1, source_target_pairs={{0,1},{1,0},{2,3},{3,2},{4,5},{5,4},{6,7},{7,6},{8,9},{9,8},{10,11... | collective-permute-start | bytes 55304 | tf_op jit(solution)/shard_map/ppermute | solution.py:521
  6.0 4.3 %collective-permute-start.3 = (f32[9,4,128]{2,1,0:T(4,128)S(1)}, f32[9,4,128]{2,1,0:T(4,128)S(1)}, u32[]{:S(2)}, u32[]{:S(2)}) collective-permute-start(f32[9,4,128]{2,1,0:T(4,128)S(1)} %get-tuple-element.22), channel_id=1, source_target_pairs={{0,4},{1,2},{2,1},{3,7},{4,0},{5,6},{6,5},{7,3},{8,12},{9,10},{10,... | collective-permute-start | bytes 55304 | tf_op jit(solution)/shard_map/ppermute | solution.py:521
  11.0 13.9 %collective-permute-start.4 = (f32[4,16,128]{2,1,0:T(8,128)S(1)}, f32[4,16,128]{2,1,0:T(8,128)S(1)}, u32[]{:S(2)}, u32[]{:S(2)}) collective-permute-start(f32[4,16,128]{2,1,0:T(8,128)S(1)} %get-tuple-element.27), channel_id=1, source_target_pairs={{0,1},{1,0},{2,3},{3,2},{4,5},{5,4},{6,7},{7,6},{8,9},{9,8},{10,11... | collective-permute-start | bytes 98312 | tf_op jit(solution)/shard_map/ppermute | solution.py:534
  11.1 13.8 %collective-permute-start.5 = (f32[4,16,128]{2,1,0:T(8,128)S(1)}, f32[4,16,128]{2,1,0:T(8,128)S(1)}, u32[]{:S(2)}, u32[]{:S(2)}) collective-permute-start(f32[4,16,128]{2,1,0:T(8,128)S(1)} %get-tuple-element.28), channel_id=1, source_target_pairs={{0,2},{1,3},{2,0},{3,1},{4,6},{5,7},{6,4},{7,5},{8,10},{9,11},{10,... | collective-permute-start | bytes 98312 | tf_op jit(solution)/shard_map/ppermute | solution.py:534
  12.2 12.7 %collective-permute-start.6 = (f32[4,16,128]{2,1,0:T(8,128)S(1)}, f32[4,16,128]{2,1,0:T(8,128)S(1)}, u32[]{:S(2)}, u32[]{:S(2)}) collective-permute-start(f32[4,16,128]{2,1,0:T(8,128)S(1)} %get-tuple-element.29), channel_id=1, source_target_pairs={{0,3},{1,2},{2,1},{3,0},{4,7},{5,6},{6,5},{7,4},{8,11},{9,10},{10,... | collective-permute-start | bytes 98312 | tf_op jit(solution)/shard_map/ppermute | solution.py:534

commit v4 on v3

--- a/solution.py
+++ b/solution.py
@@ -271,22 +271,15 @@
     xb_ref,
     ya_ref,
     yb_ref,
-    blocks_hbm,
-    owners_hbm,
-    targets_hbm,
+    blocks_ref,
+    owners_ref,
+    targets_ref,
     *refs,
 ):
     width_x, width_y, depth_z = sizes
     out_ref, goal_ref = refs[:2]
     send_refs = refs[2 : 2 + count_py]
-    sending, blocks_ref, owners_ref, targets_ref, sems = refs[2 + count_py :]
-    copies = [
-        pltpu.make_async_copy(blocks_hbm, blocks_ref, sems.at[0]),
-        pltpu.make_async_copy(owners_hbm, owners_ref, sems.at[1]),
-        pltpu.make_async_copy(targets_hbm, targets_ref, sems.at[2]),
-    ]
-    for copy in copies:
-        copy.start()
+    (sending,) = refs[2 + count_py :]
     lane = lax.broadcasted_iota(jnp.int32, (width_y, depth_z), 1)
     row = lax.broadcasted_iota(jnp.int32, (width_y, depth_z), 0)
     index_x = lax.axis_index("px")
@@ -398,13 +391,12 @@
             for corner in range(8):
                 out_ref[field * 8 + corner, x] = result[corner]
         lower_x = upper_x
-    for copy in copies:
-        copy.wait()
     half = lax.broadcasted_iota(jnp.int32, goal_ref.shape, 1) < depth_z // 2
-    goal_ref[...] = jnp.where(half, targets_ref[0], targets_ref[1])
+    goal_ref[...] = jnp.where(half, targets_ref[:, 0:1], targets_ref[:, 1:2])
     place = index_y
+    owners_row, blocks_row = owners_ref[...], blocks_ref[...]
     rows = out_ref.reshape(16 * width_x * width_y, depth_z)
-    owners = [owners_ref[0, entry] for entry in range(entries)]
+    owners = [owners_row[0, entry] for entry in range(entries)]
     for entry in range(entries):
         slot = jnp.int32(0)
         for earlier in range(entry):
@@ -414,7 +406,7 @@
         else:
             hop = lax.rem(owners[entry] - place + count_py, count_py)
         sending[hop * capacity + slot] = rows[
-            pl.ds(blocks_ref[0, entry], 16, stride=width_x * width_y), :
+            pl.ds(blocks_row[0, entry], 16, stride=width_x * width_y), :
         ]
     for hop in range(count_py):
         send_refs[hop][...] = sending[pl.ds(hop * capacity, capacity)]
@@ -437,18 +429,14 @@
         functools.partial(remap_kernel, sizes, count_py, entries, capacity),
         out_shape=(shape_of(16, *sizes), shape_of(1, depth_z))
         + (shape_of(capacity, 16, depth_z),) * count_py,
-        in_specs=[in_vmem()] * 6 + [in_place()] * 3,
+        in_specs=[in_vmem()] * 9,
         out_specs=(in_vmem(),) * (2 + count_py),
         scratch_shapes=[
             pltpu.VMEM((count_py * capacity, 16, depth_z), jnp.float32),
-            pltpu.SMEM(blocks.shape, jnp.int32),
-            pltpu.SMEM(owners.shape, jnp.int32),
-            pltpu.SMEM(targets.shape, jnp.float32),
-            pltpu.SemaphoreType.DMA((3,)),
         ],
         compiler_params=kernel_options(),
         name="remap",
-    )(state, relative, *halos, blocks, owners, targets)
+    )(state, relative, *halos, blocks, owners, targets.reshape(1, 2))
 
 
 def finish_kernel(total_nodes, count_py, capacity, state_ref, total_ref, goal_ref, *refs):

time: 26 us -> 25.7 us (0.988)
  Pallas kernels: 3.47 us -> 3.15 us
    pallas_call x1, Pallas kernels: 0.7 us -> 0.38 us  [remap_call(): pl.pallas_call(functools.partial(remap_kernel, sizes, count_py, entries,...]
where the time goes in v4:
time: 25.7 us; the launch traced here: 25.6 us
  blocking collectives  12 us (47%)
  starting transfers between devices  7.99 us (31%)
  Pallas kernels  3.15 us (12%)
  waiting for transfers between devices  1.75 us (7%)
  between operations  0.7 us (3%)
    all_to_all x1, blocking collectives, step(): gathered = lax.all_to_all(total, ('px', 'py'), 0, 0, tiled=True)  12 us
    ppermute x4, starting transfers between devices, step(): lax.ppermute(message, ('px', 'py'), exchanges(counts, axis, first))  6.07 us
    ppermute x3, starting transfers between devices, step(): received.append(lax.ppermute(chunks[hop], 'py', hop_pairs(count_py, hop)))  1.92 us
    pallas_call x1, Pallas kernels, lagrange_call(): pl.pallas_call(functools.partial(lagrange_kernel, sizes), out_shape=(shap...  1.8 us
    ppermute x4, waiting for transfers between devices, step(): lax.ppermute(message, ('px', 'py'), exchanges(counts, axis, first))  1.74 us
    pallas_call x1, Pallas kernels, finish_call(): pl.pallas_call(functools.partial(finish_kernel, total_nodes, count_py, ca...  0.97 us
  transfers between devices with their start and end apart: 7, of which 1 were waited for; matrix products, arithmetic and copies ran while one was open for 0% of the time, Pallas kernels for 0%

profile of v4, /device:TPU:0, one launch (start us, length us, event | category | flops | bytes accessed | tf_op | source)
XLA Modules:
  0.0 25.6 jit_solution(2261592868497851747)
XLA Ops:
  0.6 0.0 copy-start.1
  0.6 0.0 copy-start
  0.7 0.0 copy-start.2
  0.7 1.8 %lagrange.1 = (f32[16,4,8,128]{3,2,1,0:T(8,128)S(1)}, f32[3,4,8,128]{3,2,1,0:T(8,128)S(1)}, f32[9,8,128]{2,1,0:T(8,128)S(1)}, f32[9,8,128]{2,1,0:T(8,128)S(1)}, ...) custom-call(f32[16,4,8,128]{3,2,1,0:T(8,128)} %bitcast.9, f32[81,4,8,128]{3,2,1,0:T(8,128)} %bitcast.8), custom_call_target="tpu_custom_call" | custom-call | tf_op jit(solution)/shard_map/lagrange/pallas_call | solution.py:235
  2.5 3.0 %collective-permute-start = (f32[9,8,128]{2,1,0:T(8,128)S(1)}, f32[9,8,128]{2,1,0:T(8,128)S(1)}, u32[]{:S(2)}, u32[]{:S(2)}) collective-permute-start(f32[9,8,128]{2,1,0:T(8,128)S(1)} %get-tuple-element.19), channel_id=1, source_target_pairs={{0,4},{1,5},{2,6},{3,7},{4,0},{5,1},{6,2},{7,3},{8,12},{9,13},{10,... | collective-permute-start | bytes 110600 | tf_op jit(solution)/shard_map/ppermute | solution.py:509
  5.5 0.0 collective-permute-start.1
  5.5 0.5 %collective-permute-start.2 = (f32[9,4,128]{2,1,0:T(4,128)S(1)}, f32[9,4,128]{2,1,0:T(4,128)S(1)}, u32[]{:S(2)}, u32[]{:S(2)}) collective-permute-start(f32[9,4,128]{2,1,0:T(4,128)S(1)} %get-tuple-element.21), channel_id=1, source_target_pairs={{0,1},{1,0},{2,3},{3,2},{4,5},{5,4},{6,7},{7,6},{8,9},{9,8},{10,11... | collective-permute-start | bytes 55304 | tf_op jit(solution)/shard_map/ppermute | solution.py:509
  6.0 2.5 %collective-permute-start.3 = (f32[9,4,128]{2,1,0:T(4,128)S(1)}, f32[9,4,128]{2,1,0:T(4,128)S(1)}, u32[]{:S(2)}, u32[]{:S(2)}) collective-permute-start(f32[9,4,128]{2,1,0:T(4,128)S(1)} %get-tuple-element.22), channel_id=1, source_target_pairs={{0,4},{1,2},{2,1},{3,7},{4,0},{5,6},{6,5},{7,3},{8,12},{9,10},{10,... | collective-permute-start | bytes 55304 | tf_op jit(solution)/shard_map/ppermute | solution.py:509
  8.5 0.0 collective-permute-done.2.ya_ref
  8.6 1.7 %collective-permute-done.3.yb_ref = f32[9,4,128]{2,1,0:T(4,128)S(1)} collective-permute-done((f32[9,4,128]{2,1,0:T(4,128)S(1)}, f32[9,4,128]{2,1,0:T(4,128)S(1)}, u32[]{:S(2)}, u32[]{:S(2)}) %collective-permute-start.3) | collective-permute-done | bytes 18464 | tf_op jit(solution)/shard_map/ppermute | solution.py:509
  10.3 0.0 collective-permute-done.xa_ref
  10.3 0.0 collective-permute-done.1.xb_ref
  10.3 0.0 copy-done.1
  10.3 0.0 copy-done
  10.3 0.0 copy-done.2
  10.3 0.4 %remap.1 = (f32[16,4,8,128]{3,2,1,0:T(8,128)S(1)}, f32[1,128]{1,0:T(1,128)S(1)}, f32[4,16,128]{2,1,0:T(8,128)S(1)}, f32[4,16,128]{2,1,0:T(8,128)S(1)}, f32[4,16,...) custom-call(f32[16,4,8,128]{3,2,1,0:T(8,128)S(1)} %get-tuple-element.17.state_ref, ...), custom_call_target="tpu_custom_call" | custom-call | tf_op jit(solution)/shard_map/remap/pallas_call | solution.py:428
  10.7 0.1 collective-permute-start.4
  10.8 1.1 %collective-permute-start.5 = (f32[4,16,128]{2,1,0:T(8,128)S(1)}, f32[4,16,128]{2,1,0:T(8,128)S(1)}, u32[]{:S(2)}, u32[]{:S(2)}) collective-permute-start(f32[4,16,128]{2,1,0:T(8,128)S(1)} %get-tuple-element.28), channel_id=1, source_target_pairs={{0,2},{1,3},{2,0},{3,1},{4,6},{5,7},{6,4},{7,5},{8,10},{9,11},{10,... | collective-permute-start | bytes 98312 | tf_op jit(solution)/shard_map/ppermute | solution.py:522
  11.9 0.7 %collective-permute-start.6 = (f32[4,16,128]{2,1,0:T(8,128)S(1)}, f32[4,16,128]{2,1,0:T(8,128)S(1)}, u32[]{:S(2)}, u32[]{:S(2)}) collective-permute-start(f32[4,16,128]{2,1,0:T(8,128)S(1)} %get-tuple-element.29), channel_id=1, source_target_pairs={{0,3},{1,2},{2,1},{3,0},{4,7},{5,6},{6,5},{7,4},{8,11},{9,10},{10,... | collective-permute-start | bytes 98312 | tf_op jit(solution)/shard_map/ppermute | solution.py:522
  12.6 12.0 %all_to_all.5.total_ref = f32[32,1,128]{2,1,0:T(1,128)S(1)} all-to-all(f32[32,1,128]{2,1,0:T(1,128)S(1)} %get-tuple-element.24), channel_id=1, replica_groups=mesh['px'=8,'py'=4] {'px','py'}, dimensions={0} | all-to-all | bytes 32768 | tf_op jit(solution)/shard_map/all_to_all | solution.py:510
  24.6 0.0 collective-permute-done.4.refs_1_
  24.6 0.0 collective-permute-done.5.refs_2_
  24.6 0.0 collective-permute-done.6.refs_3_
  24.6 1.0 %finish.1 = (f32[16,4,8,128]{3,2,1,0:T(8,128)}, f32[16,16,128]{2,1,0:T(8,128)}) custom-call(f32[16,4,8,128]{3,2,1,0:T(8,128)S(1)} %get-tuple-element.23.state_ref, f32[32,1,128]{2,1,0:T(1,128)S(1)} %all_to_all.5.total_ref, f32[1,128]{1,0:T(1,128)S(1)} %get-tuple-element.25.goal_ref, f32[4,16,128]{2,1,0:T(8,128)S(1)} %get-tuple-element.26.refs_0_, ...), custom_call_target="tpu_custom_call" | custom-call | tf_op jit(solution)/shard_map/finish/pallas_call | solution.py:479
Async XLA Ops:
  0.6 9.7 %copy-start.1 = (s32[1,8,1]{1,2,0:T(1,128)S(1)}, s32[1,8,1]{1,2,0:T(1,128)}, u32[]{:S(2)}) copy-start(s32[1,8,1]{1,2,0:T(1,128)} %param.9) | copy-start | bytes 100
  0.6 9.7 %copy-start = (s32[1,8]{1,0:T(1,128)S(1)}, s32[1,8]{1,0:T(1,128)}, u32[]{:S(2)}) copy-start(s32[1,8]{1,0:T(1,128)} %blocks_ref.1) | copy-start | bytes 100
  0.7 9.7 %copy-start.2 = (f32[2]{0:T(128)S(1)}, f32[2]{0:T(128)}, u32[]{:S(2)}) copy-start(f32[2]{0:T(128)} %param.7) | copy-start | bytes 28
  2.5 7.8 %collective-permute-start = (f32[9,8,128]{2,1,0:T(8,128)S(1)}, f32[9,8,128]{2,1,0:T(8,128)S(1)}, u32[]{:S(2)}, u32[]{:S(2)}) collective-permute-start(f32[9,8,128]{2,1,0:T(8,128)S(1)} %get-tuple-element.19), channel_id=1, source_target_pairs={{0,4},{1,5},{2,6},{3,7},{4,0},{5,1},{6,2},{7,3},{8,12},{9,13},{10,... | collective-permute-start | bytes 110600 | tf_op jit(solution)/shard_map/ppermute | solution.py:509
  5.5 4.8 %collective-permute-start.1 = (f32[9,8,128]{2,1,0:T(8,128)S(1)}, f32[9,8,128]{2,1,0:T(8,128)S(1)}, u32[]{:S(2)}, u32[]{:S(2)}) collective-permute-start(f32[9,8,128]{2,1,0:T(8,128)S(1)} %get-tuple-element.20), channel_id=1, source_target_pairs={{0,1},{1,0},{2,3},{3,2},{4,8},{5,9},{6,10},{7,11},{8,4},{9,5},{10,... | collective-permute-start | bytes 110600 | tf_op jit(solution)/shard_map/ppermute | solution.py:509
  5.5 3.0 %collective-permute-start.2 = (f32[9,4,128]{2,1,0:T(4,128)S(1)}, f32[9,4,128]{2,1,0:T(4,128)S(1)}, u32[]{:S(2)}, u32[]{:S(2)}) collective-permute-start(f32[9,4,128]{2,1,0:T(4,128)S(1)} %get-tuple-element.21), channel_id=1, source_target_pairs={{0,1},{1,0},{2,3},{3,2},{4,5},{5,4},{6,7},{7,6},{8,9},{9,8},{10,11... | collective-permute-start | bytes 55304 | tf_op jit(solution)/shard_map/ppermute | solution.py:509
  6.0 4.3 %collective-permute-start.3 = (f32[9,4,128]{2,1,0:T(4,128)S(1)}, f32[9,4,128]{2,1,0:T(4,128)S(1)}, u32[]{:S(2)}, u32[]{:S(2)}) collective-permute-start(f32[9,4,128]{2,1,0:T(4,128)S(1)} %get-tuple-element.22), channel_id=1, source_target_pairs={{0,4},{1,2},{2,1},{3,7},{4,0},{5,6},{6,5},{7,3},{8,12},{9,10},{10,... | collective-permute-start | bytes 55304 | tf_op jit(solution)/shard_map/ppermute | solution.py:509
  10.7 13.9 %collective-permute-start.4 = (f32[4,16,128]{2,1,0:T(8,128)S(1)}, f32[4,16,128]{2,1,0:T(8,128)S(1)}, u32[]{:S(2)}, u32[]{:S(2)}) collective-permute-start(f32[4,16,128]{2,1,0:T(8,128)S(1)} %get-tuple-element.27), channel_id=1, source_target_pairs={{0,1},{1,0},{2,3},{3,2},{4,5},{5,4},{6,7},{7,6},{8,9},{9,8},{10,11... | collective-permute-start | bytes 98312 | tf_op jit(solution)/shard_map/ppermute | solution.py:522
  10.8 13.8 %collective-permute-start.5 = (f32[4,16,128]{2,1,0:T(8,128)S(1)}, f32[4,16,128]{2,1,0:T(8,128)S(1)}, u32[]{:S(2)}, u32[]{:S(2)}) collective-permute-start(f32[4,16,128]{2,1,0:T(8,128)S(1)} %get-tuple-element.28), channel_id=1, source_target_pairs={{0,2},{1,3},{2,0},{3,1},{4,6},{5,7},{6,4},{7,5},{8,10},{9,11},{10,... | collective-permute-start | bytes 98312 | tf_op jit(solution)/shard_map/ppermute | solution.py:522
  11.9 12.7 %collective-permute-start.6 = (f32[4,16,128]{2,1,0:T(8,128)S(1)}, f32[4,16,128]{2,1,0:T(8,128)S(1)}, u32[]{:S(2)}, u32[]{:S(2)}) collective-permute-start(f32[4,16,128]{2,1,0:T(8,128)S(1)} %get-tuple-element.29), channel_id=1, source_target_pairs={{0,3},{1,2},{2,1},{3,0},{4,7},{5,6},{6,5},{7,4},{8,11},{9,10},{10,... | collective-permute-start | bytes 98312 | tf_op jit(solution)/shard_map/ppermute | solution.py:522

commit v5 on v4

--- a/solution.py
+++ b/solution.py
@@ -45,6 +45,10 @@
     return pairs
 
 
+def swaps(size):
+    return [(i, i ^ 1 if i ^ 1 < size else i) for i in range(size)]
+
+
 def giver_of(index, hop, size):
     if size & (size - 1) == 0:
         return index ^ hop
@@ -96,12 +100,10 @@
     xb_ref,
     ya_ref,
     yb_ref,
-    total_hbm,
+    total_ref,
     motion_ref,
-    total_ref,
     state_sem,
     motion_sem,
-    total_sem,
 ):
     width_x, width_y, depth_z = sizes
     copies = []
@@ -203,8 +205,6 @@
                     part = part - leaving[direction] * high
             totals[field] = part if totals[field] is None else totals[field] + part
     total_ref[...] = jnp.broadcast_to(folded(totals)[None], total_ref.shape)
-    total_copy = pltpu.make_async_copy(total_ref, total_hbm, total_sem)
-    total_copy.start()
     odd_x = lax.rem(index_x, 2)
     for out_ref, side in ((xa_ref, 1 - odd_x), (xb_ref, odd_x)):
         place = side * (width_x - 1)
@@ -226,7 +226,6 @@
                         pl.ds(start, width_x, stride=width_y), :
                     ]
         out_ref[8] = relative_rows[pl.ds(column + place, width_x, stride=width_y), :]
-    total_copy.wait()
 
 
 def lagrange_call(conserved, velocity, device_count):
@@ -244,13 +243,11 @@
             shape_of(device_count, 1, depth_z),
         ),
         in_specs=[in_place()] * 2,
-        out_specs=(in_vmem(),) * 6 + (in_place(),),
+        out_specs=(in_vmem(),) * 7,
         scratch_shapes=[
             pltpu.VMEM((81,) + sizes, jnp.float32),
-            pltpu.VMEM((device_count, 1, depth_z), jnp.float32),
             pltpu.SemaphoreType.DMA((width_x,)),
             pltpu.SemaphoreType.DMA((width_x,)),
-            pltpu.SemaphoreType.DMA,
         ],
         compiler_params=kernel_options(),
         name="lagrange",
@@ -507,6 +504,7 @@
     halos = []
     for message, axis, first in ((xa, 0, 0), (xb, 0, 1), (ya, 1, 0), (yb, 1, 1)):
         halos.append(lax.ppermute(message, ("px", "py"), exchanges(counts, axis, first)))
+    total = lax.ppermute(total, "py", swaps(count_py))
     gathered = lax.all_to_all(total, ("px", "py"), 0, 0, tiled=True)
     remapped, goal, *chunks = remap_call(
         state,

time: 25.7 us -> 25.7 us (level)
  transfers between devices with their start and end apart: 7 -> 8, of which waited for: 1 -> 1; matrix products, arithmetic and copies ran while one was open for 0% -> 0% of each run, Pallas kernels for 0% -> 1%
where the time goes in v5:
time: 25.7 us; the launch traced here: 25.5 us
  blocking collectives  12 us (47%)
  starting transfers between devices  7.99 us (31%)
  Pallas kernels  3.1 us (12%)
  waiting for transfers between devices  1.75 us (7%)
  between operations  0.7 us (3%)
    all_to_all x1, blocking collectives, step(): gathered = lax.all_to_all(total, ('px', 'py'), 0, 0, tiled=True)  12 us
    ppermute x4, starting transfers between devices, step(): lax.ppermute(message, ('px', 'py'), exchanges(counts, axis, first))  6.07 us
    ppermute x3, starting transfers between devices, step(): received.append(lax.ppermute(chunks[hop], 'py', hop_pairs(count_py, hop)))  1.92 us
    pallas_call x1, Pallas kernels, lagrange_call(): pl.pallas_call(functools.partial(lagrange_kernel, sizes), out_shape=(shap...  1.76 us
    ppermute x4, waiting for transfers between devices, step(): lax.ppermute(message, ('px', 'py'), exchanges(counts, axis, first))  1.74 us
    pallas_call x1, Pallas kernels, finish_call(): pl.pallas_call(functools.partial(finish_kernel, total_nodes, count_py, ca...  0.97 us
  transfers between devices with their start and end apart: 8, of which 1 were waited for; matrix products, arithmetic and copies ran while one was open for 0% of the time, Pallas kernels for 1%

profile of v5, /device:TPU:0, one launch (start us, length us, event | category | flops | bytes accessed | tf_op | source)
XLA Modules:
  0.0 25.5 jit_solution(1240515401101022993)
XLA Ops:
  0.6 0.0 copy-start.1
  0.6 0.0 copy-start
  0.7 0.0 copy-start.2
  0.7 1.8 %lagrange.1 = (f32[16,4,8,128]{3,2,1,0:T(8,128)S(1)}, f32[3,4,8,128]{3,2,1,0:T(8,128)S(1)}, f32[9,8,128]{2,1,0:T(8,128)S(1)}, f32[9,8,128]{2,1,0:T(8,128)S(1)}, ...) custom-call(f32[16,4,8,128]{3,2,1,0:T(8,128)} %bitcast.9, f32[81,4,8,128]{3,2,1,0:T(8,128)} %bitcast.8), custom_call_target="tpu_custom_call" | custom-call | tf_op jit(solution)/shard_map/lagrange/pallas_call | solution.py:234
  2.4 3.0 %collective-permute-start = (f32[9,8,128]{2,1,0:T(8,128)S(1)}, f32[9,8,128]{2,1,0:T(8,128)S(1)}, u32[]{:S(2)}, u32[]{:S(2)}) collective-permute-start(f32[9,8,128]{2,1,0:T(8,128)S(1)} %get-tuple-element.19), channel_id=1, source_target_pairs={{0,4},{1,5},{2,6},{3,7},{4,0},{5,1},{6,2},{7,3},{8,12},{9,13},{10,... | collective-permute-start | bytes 110600 | tf_op jit(solution)/shard_map/ppermute | solution.py:506
  5.5 0.0 collective-permute-start.1
  5.5 0.5 %collective-permute-start.2 = (f32[9,4,128]{2,1,0:T(4,128)S(1)}, f32[9,4,128]{2,1,0:T(4,128)S(1)}, u32[]{:S(2)}, u32[]{:S(2)}) collective-permute-start(f32[9,4,128]{2,1,0:T(4,128)S(1)} %get-tuple-element.21), channel_id=1, source_target_pairs={{0,1},{1,0},{2,3},{3,2},{4,5},{5,4},{6,7},{7,6},{8,9},{9,8},{10,11... | collective-permute-start | bytes 55304 | tf_op jit(solution)/shard_map/ppermute | solution.py:506
  6.0 2.5 %collective-permute-start.3 = (f32[9,4,128]{2,1,0:T(4,128)S(1)}, f32[9,4,128]{2,1,0:T(4,128)S(1)}, u32[]{:S(2)}, u32[]{:S(2)}) collective-permute-start(f32[9,4,128]{2,1,0:T(4,128)S(1)} %get-tuple-element.22), channel_id=1, source_target_pairs={{0,4},{1,2},{2,1},{3,7},{4,0},{5,6},{6,5},{7,3},{8,12},{9,10},{10,... | collective-permute-start | bytes 55304 | tf_op jit(solution)/shard_map/ppermute | solution.py:506
  8.5 0.0 collective-permute-start.4
  8.5 0.0 collective-permute-done.2.ya_ref
  8.5 1.7 %collective-permute-done.3.yb_ref = f32[9,4,128]{2,1,0:T(4,128)S(1)} collective-permute-done((f32[9,4,128]{2,1,0:T(4,128)S(1)}, f32[9,4,128]{2,1,0:T(4,128)S(1)}, u32[]{:S(2)}, u32[]{:S(2)}) %collective-permute-start.3) | collective-permute-done | bytes 18464 | tf_op jit(solution)/shard_map/ppermute | solution.py:506
  10.2 0.0 collective-permute-done.xa_ref
  10.2 0.0 collective-permute-done.1.xb_ref
  10.2 0.0 copy-done.1
  10.3 0.0 copy-done
  10.3 0.0 copy-done.2
  10.3 0.4 %remap.1 = (f32[16,4,8,128]{3,2,1,0:T(8,128)S(1)}, f32[1,128]{1,0:T(1,128)S(1)}, f32[4,16,128]{2,1,0:T(8,128)S(1)}, f32[4,16,128]{2,1,0:T(8,128)S(1)}, f32[4,16,...) custom-call(f32[16,4,8,128]{3,2,1,0:T(8,128)S(1)} %get-tuple-element.17.state_ref, ...), custom_call_target="tpu_custom_call" | custom-call | tf_op jit(solution)/shard_map/remap/pallas_call | solution.py:425
  10.7 0.1 collective-permute-start.5
  10.7 1.1 %collective-permute-start.6 = (f32[4,16,128]{2,1,0:T(8,128)S(1)}, f32[4,16,128]{2,1,0:T(8,128)S(1)}, u32[]{:S(2)}, u32[]{:S(2)}) collective-permute-start(f32[4,16,128]{2,1,0:T(8,128)S(1)} %get-tuple-element.28), channel_id=1, source_target_pairs={{0,2},{1,3},{2,0},{3,1},{4,6},{5,7},{6,4},{7,5},{8,10},{9,11},{10,... | collective-permute-start | bytes 98312 | tf_op jit(solution)/shard_map/ppermute | solution.py:520
  11.9 0.7 %collective-permute-start.7 = (f32[4,16,128]{2,1,0:T(8,128)S(1)}, f32[4,16,128]{2,1,0:T(8,128)S(1)}, u32[]{:S(2)}, u32[]{:S(2)}) collective-permute-start(f32[4,16,128]{2,1,0:T(8,128)S(1)} %get-tuple-element.29), channel_id=1, source_target_pairs={{0,3},{1,2},{2,1},{3,0},{4,7},{5,6},{6,5},{7,4},{8,11},{9,10},{10,... | collective-permute-start | bytes 98312 | tf_op jit(solution)/shard_map/ppermute | solution.py:520
  12.6 0.0 collective-permute-done.4
  12.6 12.0 %all_to_all.5.total_ref = f32[32,1,128]{2,1,0:T(1,128)S(1)} all-to-all(f32[32,1,128]{2,1,0:T(1,128)S(1)} %collective-permute-done.4), channel_id=1, replica_groups=mesh['px'=8,'py'=4] {'px','py'}, dimensions={0} | all-to-all | bytes 32768 | tf_op jit(solution)/shard_map/all_to_all | solution.py:508
  24.5 0.0 collective-permute-done.5.refs_1_
  24.5 0.0 collective-permute-done.6.refs_2_
  24.5 0.0 collective-permute-done.7.refs_3_
  24.6 1.0 %finish.1 = (f32[16,4,8,128]{3,2,1,0:T(8,128)}, f32[16,16,128]{2,1,0:T(8,128)}) custom-call(f32[16,4,8,128]{3,2,1,0:T(8,128)S(1)} %get-tuple-element.23.state_ref, f32[32,1,128]{2,1,0:T(1,128)S(1)} %all_to_all.5.total_ref, f32[1,128]{1,0:T(1,128)S(1)} %get-tuple-element.25.goal_ref, f32[4,16,128]{2,1,0:T(8,128)S(1)} %get-tuple-element.26.refs_0_, ...), custom_call_target="tpu_custom_call" | custom-call | tf_op jit(solution)/shard_map/finish/pallas_call | solution.py:476
Async XLA Ops:
  0.6 9.6 %copy-start.1 = (s32[1,8,1]{1,2,0:T(1,128)S(1)}, s32[1,8,1]{1,2,0:T(1,128)}, u32[]{:S(2)}) copy-start(s32[1,8,1]{1,2,0:T(1,128)} %param.9) | copy-start | bytes 100
  0.6 9.6 %copy-start = (s32[1,8]{1,0:T(1,128)S(1)}, s32[1,8]{1,0:T(1,128)}, u32[]{:S(2)}) copy-start(s32[1,8]{1,0:T(1,128)} %blocks_ref.1) | copy-start | bytes 100
  0.7 9.6 %copy-start.2 = (f32[2]{0:T(128)S(1)}, f32[2]{0:T(128)}, u32[]{:S(2)}) copy-start(f32[2]{0:T(128)} %param.7) | copy-start | bytes 28
  2.4 7.8 %collective-permute-start = (f32[9,8,128]{2,1,0:T(8,128)S(1)}, f32[9,8,128]{2,1,0:T(8,128)S(1)}, u32[]{:S(2)}, u32[]{:S(2)}) collective-permute-start(f32[9,8,128]{2,1,0:T(8,128)S(1)} %get-tuple-element.19), channel_id=1, source_target_pairs={{0,4},{1,5},{2,6},{3,7},{4,0},{5,1},{6,2},{7,3},{8,12},{9,13},{10,... | collective-permute-start | bytes 110600 | tf_op jit(solution)/shard_map/ppermute | solution.py:506
  5.5 4.8 %collective-permute-start.1 = (f32[9,8,128]{2,1,0:T(8,128)S(1)}, f32[9,8,128]{2,1,0:T(8,128)S(1)}, u32[]{:S(2)}, u32[]{:S(2)}) collective-permute-start(f32[9,8,128]{2,1,0:T(8,128)S(1)} %get-tuple-element.20), channel_id=1, source_target_pairs={{0,1},{1,0},{2,3},{3,2},{4,8},{5,9},{6,10},{7,11},{8,4},{9,5},{10,... | collective-permute-start | bytes 110600 | tf_op jit(solution)/shard_map/ppermute | solution.py:506
  5.5 3.0 %collective-permute-start.2 = (f32[9,4,128]{2,1,0:T(4,128)S(1)}, f32[9,4,128]{2,1,0:T(4,128)S(1)}, u32[]{:S(2)}, u32[]{:S(2)}) collective-permute-start(f32[9,4,128]{2,1,0:T(4,128)S(1)} %get-tuple-element.21), channel_id=1, source_target_pairs={{0,1},{1,0},{2,3},{3,2},{4,5},{5,4},{6,7},{7,6},{8,9},{9,8},{10,11... | collective-permute-start | bytes 55304 | tf_op jit(solution)/shard_map/ppermute | solution.py:506
  6.0 4.3 %collective-permute-start.3 = (f32[9,4,128]{2,1,0:T(4,128)S(1)}, f32[9,4,128]{2,1,0:T(4,128)S(1)}, u32[]{:S(2)}, u32[]{:S(2)}) collective-permute-start(f32[9,4,128]{2,1,0:T(4,128)S(1)} %get-tuple-element.22), channel_id=1, source_target_pairs={{0,4},{1,2},{2,1},{3,7},{4,0},{5,6},{6,5},{7,3},{8,12},{9,10},{10,... | collective-permute-start | bytes 55304 | tf_op jit(solution)/shard_map/ppermute | solution.py:506
  8.5 4.1 %collective-permute-start.4 = (f32[32,1,128]{2,1,0:T(1,128)S(1)}, f32[32,1,128]{2,1,0:T(1,128)S(1)}, u32[]{:S(2)}, u32[]{:S(2)}) collective-permute-start(f32[32,1,128]{2,1,0:T(1,128)S(1)} %get-tuple-element.24), channel_id=1, source_target_pairs={{0,1},{1,0},{2,3},{3,2},{4,5},{5,4},{6,7},{7,6},{8,9},{9,8},{10,11... | collective-permute-start | bytes 49160 | tf_op jit(solution)/shard_map/ppermute | solution.py:507
  10.7 13.9 %collective-permute-start.5 = (f32[4,16,128]{2,1,0:T(8,128)S(1)}, f32[4,16,128]{2,1,0:T(8,128)S(1)}, u32[]{:S(2)}, u32[]{:S(2)}) collective-permute-start(f32[4,16,128]{2,1,0:T(8,128)S(1)} %get-tuple-element.27), channel_id=1, source_target_pairs={{0,1},{1,0},{2,3},{3,2},{4,5},{5,4},{6,7},{7,6},{8,9},{9,8},{10,11... | collective-permute-start | bytes 98312 | tf_op jit(solution)/shard_map/ppermute | solution.py:520
  10.7 13.8 %collective-permute-start.6 = (f32[4,16,128]{2,1,0:T(8,128)S(1)}, f32[4,16,128]{2,1,0:T(8,128)S(1)}, u32[]{:S(2)}, u32[]{:S(2)}) collective-permute-start(f32[4,16,128]{2,1,0:T(8,128)S(1)} %get-tuple-element.28), channel_id=1, source_target_pairs={{0,2},{1,3},{2,0},{3,1},{4,6},{5,7},{6,4},{7,5},{8,10},{9,11},{10,... | collective-permute-start | bytes 98312 | tf_op jit(solution)/shard_map/ppermute | solution.py:520
  11.9 12.7 %collective-permute-start.7 = (f32[4,16,128]{2,1,0:T(8,128)S(1)}, f32[4,16,128]{2,1,0:T(8,128)S(1)}, u32[]{:S(2)}, u32[]{:S(2)}) collective-permute-start(f32[4,16,128]{2,1,0:T(8,128)S(1)} %get-tuple-element.29), channel_id=1, source_target_pairs={{0,3},{1,2},{2,1},{3,0},{4,7},{5,6},{6,5},{7,4},{8,11},{9,10},{10,... | collective-permute-start | bytes 98312 | tf_op jit(solution)/shard_map/ppermute | solution.py:520

commit v6 on v5

--- a/solution.py
+++ b/solution.py
@@ -438,7 +438,7 @@
 
 def finish_kernel(total_nodes, count_py, capacity, state_ref, total_ref, goal_ref, *refs):
     chunk_refs = refs[:count_py]
-    fixed_hbm, handed_hbm, fixed_ref, handed_ref, sems = refs[count_py:]
+    fixed_ref, handed_ref = refs[count_py:]
     total = jnp.sum(total_ref[...], axis=0)
     half = lax.broadcasted_iota(jnp.int32, total.shape, 1) < total.shape[1] // 2
     sums = (
@@ -449,12 +449,9 @@
     scale = goal_ref[...] / means
     other = pltpu.roll(scale, scale.shape[1] // 2, 1)
     factors = (jnp.where(half, scale, other), jnp.where(half, other, scale))
-    copies = []
     for field in range(2):
         part = pl.ds(field * 8, 8)
         fixed_ref[part] = state_ref[part] * factors[field]
-        copies.append(pltpu.make_async_copy(fixed_ref.at[part], fixed_hbm.at[part], sems.at[field]))
-        copies[-1].start()
     place = lax.axis_index("py")
     for hop in range(count_py):
         start = giver_of(place, hop, count_py) * capacity
@@ -463,10 +460,6 @@
             handed_ref[pl.ds(start, capacity), part, :] = (
                 chunk_refs[hop][:, part, :] * factors[field]
             )
-    copies.append(pltpu.make_async_copy(handed_ref, handed_hbm, sems.at[2]))
-    copies[-1].start()
-    for copy in copies:
-        copy.wait()
 
 
 def finish_call(state, gathered, goal, chunks, total_nodes):
@@ -477,12 +470,7 @@
         functools.partial(finish_kernel, total_nodes, count_py, capacity),
         out_shape=(shape_of(*state.shape), shape_of(*handed)),
         in_specs=[in_vmem()] * (3 + count_py),
-        out_specs=(in_place(),) * 2,
-        scratch_shapes=[
-            pltpu.VMEM(state.shape, jnp.float32),
-            pltpu.VMEM(handed, jnp.float32),
-            pltpu.SemaphoreType.DMA((3,)),
-        ],
+        out_specs=(in_vmem(),) * 2,
         compiler_params=kernel_options(),
         name="finish",
     )(state, gathered, goal, *chunks)

time: 25.7 us -> 25.7 us (level)
  no operation moved by 1% of the time
where the time goes in v6:
time: 25.7 us; the launch traced here: 25.5 us
  blocking collectives  12 us (47%)
  starting transfers between devices  7.99 us (31%)
  Pallas kernels  3.09 us (12%)
  waiting for transfers between devices  1.75 us (7%)
  between operations  0.7 us (3%)
    all_to_all x1, blocking collectives, step(): gathered = lax.all_to_all(total, ('px', 'py'), 0, 0, tiled=True)  12 us
    ppermute x4, starting transfers between devices, step(): lax.ppermute(message, ('px', 'py'), exchanges(counts, axis, first))  6.07 us
    ppermute x3, starting transfers between devices, step(): received.append(lax.ppermute(chunks[hop], 'py', hop_pairs(count_py, hop)))  1.92 us
    pallas_call x1, Pallas kernels, lagrange_call(): pl.pallas_call(functools.partial(lagrange_kernel, sizes), out_shape=(shap...  1.76 us
    ppermute x4, waiting for transfers between devices, step(): lax.ppermute(message, ('px', 'py'), exchanges(counts, axis, first))  1.74 us
    pallas_call x1, Pallas kernels, finish_call(): pl.pallas_call(functools.partial(finish_kernel, total_nodes, count_py, ca...  0.95 us
  transfers between devices with their start and end apart: 8, of which 1 were waited for; matrix products, arithmetic and copies ran while one was open for 0% of the time, Pallas kernels for 1%

profile of v6, /device:TPU:0, one launch (start us, length us, event | category | flops | bytes accessed | tf_op | source)
XLA Modules:
  0.0 25.5 jit_solution(14478298560747900261)
XLA Ops:
  0.6 0.0 copy-start.1
  0.6 0.0 copy-start
  0.7 0.0 copy-start.2
  0.7 1.8 %lagrange.1 = (f32[16,4,8,128]{3,2,1,0:T(8,128)S(1)}, f32[3,4,8,128]{3,2,1,0:T(8,128)S(1)}, f32[9,8,128]{2,1,0:T(8,128)S(1)}, f32[9,8,128]{2,1,0:T(8,128)S(1)}, ...) custom-call(f32[16,4,8,128]{3,2,1,0:T(8,128)} %bitcast.9, f32[81,4,8,128]{3,2,1,0:T(8,128)} %bitcast.8), custom_call_target="tpu_custom_call" | custom-call | tf_op jit(solution)/shard_map/lagrange/pallas_call | solution.py:234
  2.4 3.0 %collective-permute-start = (f32[9,8,128]{2,1,0:T(8,128)S(1)}, f32[9,8,128]{2,1,0:T(8,128)S(1)}, u32[]{:S(2)}, u32[]{:S(2)}) collective-permute-start(f32[9,8,128]{2,1,0:T(8,128)S(1)} %get-tuple-element.19), channel_id=1, source_target_pairs={{0,4},{1,5},{2,6},{3,7},{4,0},{5,1},{6,2},{7,3},{8,12},{9,13},{10,... | collective-permute-start | bytes 110600 | tf_op jit(solution)/shard_map/ppermute | solution.py:494
  5.5 0.0 collective-permute-start.1
  5.5 0.5 %collective-permute-start.2 = (f32[9,4,128]{2,1,0:T(4,128)S(1)}, f32[9,4,128]{2,1,0:T(4,128)S(1)}, u32[]{:S(2)}, u32[]{:S(2)}) collective-permute-start(f32[9,4,128]{2,1,0:T(4,128)S(1)} %get-tuple-element.21), channel_id=1, source_target_pairs={{0,1},{1,0},{2,3},{3,2},{4,5},{5,4},{6,7},{7,6},{8,9},{9,8},{10,11... | collective-permute-start | bytes 55304 | tf_op jit(solution)/shard_map/ppermute | solution.py:494
  6.0 2.5 %collective-permute-start.3 = (f32[9,4,128]{2,1,0:T(4,128)S(1)}, f32[9,4,128]{2,1,0:T(4,128)S(1)}, u32[]{:S(2)}, u32[]{:S(2)}) collective-permute-start(f32[9,4,128]{2,1,0:T(4,128)S(1)} %get-tuple-element.22), channel_id=1, source_target_pairs={{0,4},{1,2},{2,1},{3,7},{4,0},{5,6},{6,5},{7,3},{8,12},{9,10},{10,... | collective-permute-start | bytes 55304 | tf_op jit(solution)/shard_map/ppermute | solution.py:494
  8.5 0.0 collective-permute-start.4
  8.5 0.0 collective-permute-done.2.ya_ref
  8.5 1.7 %collective-permute-done.3.yb_ref = f32[9,4,128]{2,1,0:T(4,128)S(1)} collective-permute-done((f32[9,4,128]{2,1,0:T(4,128)S(1)}, f32[9,4,128]{2,1,0:T(4,128)S(1)}, u32[]{:S(2)}, u32[]{:S(2)}) %collective-permute-start.3) | collective-permute-done | bytes 18464 | tf_op jit(solution)/shard_map/ppermute | solution.py:494
  10.2 0.0 collective-permute-done.xa_ref
  10.2 0.0 collective-permute-done.1.xb_ref
  10.2 0.0 copy-done.1
  10.3 0.0 copy-done
  10.3 0.0 copy-done.2
  10.3 0.4 %remap.1 = (f32[16,4,8,128]{3,2,1,0:T(8,128)S(1)}, f32[1,128]{1,0:T(1,128)S(1)}, f32[4,16,128]{2,1,0:T(8,128)S(1)}, f32[4,16,128]{2,1,0:T(8,128)S(1)}, f32[4,16,...) custom-call(f32[16,4,8,128]{3,2,1,0:T(8,128)S(1)} %get-tuple-element.17.state_ref, ...), custom_call_target="tpu_custom_call" | custom-call | tf_op jit(solution)/shard_map/remap/pallas_call | solution.py:425
  10.7 0.1 collective-permute-start.5
  10.7 1.1 %collective-permute-start.6 = (f32[4,16,128]{2,1,0:T(8,128)S(1)}, f32[4,16,128]{2,1,0:T(8,128)S(1)}, u32[]{:S(2)}, u32[]{:S(2)}) collective-permute-start(f32[4,16,128]{2,1,0:T(8,128)S(1)} %get-tuple-element.28), channel_id=1, source_target_pairs={{0,2},{1,3},{2,0},{3,1},{4,6},{5,7},{6,4},{7,5},{8,10},{9,11},{10,... | collective-permute-start | bytes 98312 | tf_op jit(solution)/shard_map/ppermute | solution.py:508
  11.9 0.7 %collective-permute-start.7 = (f32[4,16,128]{2,1,0:T(8,128)S(1)}, f32[4,16,128]{2,1,0:T(8,128)S(1)}, u32[]{:S(2)}, u32[]{:S(2)}) collective-permute-start(f32[4,16,128]{2,1,0:T(8,128)S(1)} %get-tuple-element.29), channel_id=1, source_target_pairs={{0,3},{1,2},{2,1},{3,0},{4,7},{5,6},{6,5},{7,4},{8,11},{9,10},{10,... | collective-permute-start | bytes 98312 | tf_op jit(solution)/shard_map/ppermute | solution.py:508
  12.6 0.0 collective-permute-done.4
  12.6 12.0 %all_to_all.5.total_ref = f32[32,1,128]{2,1,0:T(1,128)S(1)} all-to-all(f32[32,1,128]{2,1,0:T(1,128)S(1)} %collective-permute-done.4), channel_id=1, replica_groups=mesh['px'=8,'py'=4] {'px','py'}, dimensions={0} | all-to-all | bytes 32768 | tf_op jit(solution)/shard_map/all_to_all | solution.py:496
  24.5 0.0 collective-permute-done.5.refs_1_
  24.5 0.0 collective-permute-done.6.refs_2_
  24.5 0.0 collective-permute-done.7.refs_3_
  24.6 1.0 %finish.1 = (f32[16,4,8,128]{3,2,1,0:T(8,128)}, f32[16,16,128]{2,1,0:T(8,128)}) custom-call(f32[16,4,8,128]{3,2,1,0:T(8,128)S(1)} %get-tuple-element.23.state_ref, f32[32,1,128]{2,1,0:T(1,128)S(1)} %all_to_all.5.total_ref, f32[1,128]{1,0:T(1,128)S(1)} %get-tuple-element.25.goal_ref, f32[4,16,128]{2,1,0:T(8,128)S(1)} %get-tuple-element.26.refs_0_, ...), custom_call_target="tpu_custom_call" | custom-call | tf_op jit(solution)/shard_map/finish/pallas_call | solution.py:469
Async XLA Ops:
  0.6 9.6 %copy-start.1 = (s32[1,8,1]{1,2,0:T(1,128)S(1)}, s32[1,8,1]{1,2,0:T(1,128)}, u32[]{:S(2)}) copy-start(s32[1,8,1]{1,2,0:T(1,128)} %param.9) | copy-start | bytes 100
  0.6 9.6 %copy-start = (s32[1,8]{1,0:T(1,128)S(1)}, s32[1,8]{1,0:T(1,128)}, u32[]{:S(2)}) copy-start(s32[1,8]{1,0:T(1,128)} %blocks_ref.1) | copy-start | bytes 100
  0.7 9.6 %copy-start.2 = (f32[2]{0:T(128)S(1)}, f32[2]{0:T(128)}, u32[]{:S(2)}) copy-start(f32[2]{0:T(128)} %param.7) | copy-start | bytes 28
  2.4 7.8 %collective-permute-start = (f32[9,8,128]{2,1,0:T(8,128)S(1)}, f32[9,8,128]{2,1,0:T(8,128)S(1)}, u32[]{:S(2)}, u32[]{:S(2)}) collective-permute-start(f32[9,8,128]{2,1,0:T(8,128)S(1)} %get-tuple-element.19), channel_id=1, source_target_pairs={{0,4},{1,5},{2,6},{3,7},{4,0},{5,1},{6,2},{7,3},{8,12},{9,13},{10,... | collective-permute-start | bytes 110600 | tf_op jit(solution)/shard_map/ppermute | solution.py:494
  5.5 4.8 %collective-permute-start.1 = (f32[9,8,128]{2,1,0:T(8,128)S(1)}, f32[9,8,128]{2,1,0:T(8,128)S(1)}, u32[]{:S(2)}, u32[]{:S(2)}) collective-permute-start(f32[9,8,128]{2,1,0:T(8,128)S(1)} %get-tuple-element.20), channel_id=1, source_target_pairs={{0,1},{1,0},{2,3},{3,2},{4,8},{5,9},{6,10},{7,11},{8,4},{9,5},{10,... | collective-permute-start | bytes 110600 | tf_op jit(solution)/shard_map/ppermute | solution.py:494
  5.5 3.0 %collective-permute-start.2 = (f32[9,4,128]{2,1,0:T(4,128)S(1)}, f32[9,4,128]{2,1,0:T(4,128)S(1)}, u32[]{:S(2)}, u32[]{:S(2)}) collective-permute-start(f32[9,4,128]{2,1,0:T(4,128)S(1)} %get-tuple-element.21), channel_id=1, source_target_pairs={{0,1},{1,0},{2,3},{3,2},{4,5},{5,4},{6,7},{7,6},{8,9},{9,8},{10,11... | collective-permute-start | bytes 55304 | tf_op jit(solution)/shard_map/ppermute | solution.py:494
  6.0 4.3 %collective-permute-start.3 = (f32[9,4,128]{2,1,0:T(4,128)S(1)}, f32[9,4,128]{2,1,0:T(4,128)S(1)}, u32[]{:S(2)}, u32[]{:S(2)}) collective-permute-start(f32[9,4,128]{2,1,0:T(4,128)S(1)} %get-tuple-element.22), channel_id=1, source_target_pairs={{0,4},{1,2},{2,1},{3,7},{4,0},{5,6},{6,5},{7,3},{8,12},{9,10},{10,... | collective-permute-start | bytes 55304 | tf_op jit(solution)/shard_map/ppermute | solution.py:494
  8.5 4.1 %collective-permute-start.4 = (f32[32,1,128]{2,1,0:T(1,128)S(1)}, f32[32,1,128]{2,1,0:T(1,128)S(1)}, u32[]{:S(2)}, u32[]{:S(2)}) collective-permute-start(f32[32,1,128]{2,1,0:T(1,128)S(1)} %get-tuple-element.24), channel_id=1, source_target_pairs={{0,1},{1,0},{2,3},{3,2},{4,5},{5,4},{6,7},{7,6},{8,9},{9,8},{10,11... | collective-permute-start | bytes 49160 | tf_op jit(solution)/shard_map/ppermute | solution.py:495
  10.7 13.9 %collective-permute-start.5 = (f32[4,16,128]{2,1,0:T(8,128)S(1)}, f32[4,16,128]{2,1,0:T(8,128)S(1)}, u32[]{:S(2)}, u32[]{:S(2)}) collective-permute-start(f32[4,16,128]{2,1,0:T(8,128)S(1)} %get-tuple-element.27), channel_id=1, source_target_pairs={{0,1},{1,0},{2,3},{3,2},{4,5},{5,4},{6,7},{7,6},{8,9},{9,8},{10,11... | collective-permute-start | bytes 98312 | tf_op jit(solution)/shard_map/ppermute | solution.py:508
  10.7 13.8 %collective-permute-start.6 = (f32[4,16,128]{2,1,0:T(8,128)S(1)}, f32[4,16,128]{2,1,0:T(8,128)S(1)}, u32[]{:S(2)}, u32[]{:S(2)}) collective-permute-start(f32[4,16,128]{2,1,0:T(8,128)S(1)} %get-tuple-element.28), channel_id=1, source_target_pairs={{0,2},{1,3},{2,0},{3,1},{4,6},{5,7},{6,4},{7,5},{8,10},{9,11},{10,... | collective-permute-start | bytes 98312 | tf_op jit(solution)/shard_map/ppermute | solution.py:508
  11.9 12.7 %collective-permute-start.7 = (f32[4,16,128]{2,1,0:T(8,128)S(1)}, f32[4,16,128]{2,1,0:T(8,128)S(1)}, u32[]{:S(2)}, u32[]{:S(2)}) collective-permute-start(f32[4,16,128]{2,1,0:T(8,128)S(1)} %get-tuple-element.29), channel_id=1, source_target_pairs={{0,3},{1,2},{2,1},{3,0},{4,7},{5,6},{6,5},{7,4},{8,11},{9,10},{10,... | collective-permute-start | bytes 98312 | tf_op jit(solution)/shard_map/ppermute | solution.py:508
